TPU v7x, 32 devices: a whole 2x2x4 slice. The times are simulated.
32 devices in a mesh: rows: 16 (over z, x, core), layer: 2 (over y).
Axes of the slice: x: 2, y: 2, z: 4, core: 2. Of those that a mesh axis runs over, the one named last changes fastest.
Arguments:
- gradients: float32 [4096, 32, 2880], P(('layer', 'rows')), parts along dimension 0, may hold values from -6 to 6
- in_basis: bfloat16 [5760, 2880], P(('layer', 'rows')), parts along dimension 0, may hold values from -0.109375 to 0.109375
- out_basis: bfloat16 [4096, 2048], P(('layer', 'rows')), parts along dimension 0, may hold values from -0.125 to 0.125
- eigen_seeds: int32 [5760, 2048], P(('layer', 'rows')), parts along dimension 0, may hold values from 0 to 63
Outputs:
- precond: float32 [4096, 92160], P('layer', 'rows'), parts along dimension 0
There are 2 independent parts, one for each index of `layer`. A program takes and returns all parts, laid end to end along the dimension named above; each array names one. Nothing has to cross between parts.
All inputs are finite; a program needn't handle non-finite values.
Results may differ from a plain program's by a relative error of at most 0.0041.
Values may be sent and summed in bfloat16 or wider, within the bound.
No kernel may reach another device: no remote copies, remote signals or barrier semaphores. Data moves between devices by JAX's collectives and lax.ppermute only.
A program may use at most 256 MiB of HBM per device.

v0:
```python
import jax
import jax.numpy as jnp
from jax import lax
from jax.sharding import PartitionSpec as P


def local(gradients, in_basis, out_basis, eigen_seeds):
    devices = lax.axis_size("rows")
    local_rows = gradients.shape[0]
    grads = gradients.shape[1]
    width_in = gradients.shape[2]
    span = width_in // devices
    grad_low = gradients.astype(jnp.bfloat16).reshape(local_rows * grads, width_in)
    full_in = lax.all_gather(in_basis, "rows", axis=0, tiled=True)
    rotated = jnp.dot(grad_low, full_in, preferred_element_type=jnp.float32)
    rotated = rotated.astype(jnp.bfloat16).reshape(local_rows, grads, devices, span)
    rotated = rotated.transpose(0, 2, 3, 1).reshape(local_rows, devices, span * grads)
    moved = lax.all_to_all(rotated, "rows", split_axis=1, concat_axis=0, tiled=True)
    width_out = moved.shape[0]
    moved = moved.reshape(width_out, span * grads)
    both = lax.dot_general(
        lax.all_gather(out_basis, "rows", axis=0, tiled=True),
        moved,
        (((0,), (0,)), ((), ())),
        preferred_element_type=jnp.float32,
    )
    eigval = jnp.exp2(eigen_seeds.astype(jnp.float32) * 0.125 - 4.0)
    denom = (eigval + 0.1).T
    result = both.reshape(width_out, span, grads) / denom[:, :, None]
    return result.reshape(width_out, span * grads)


def solution(mesh):
    placed = (
        P(("layer", "rows"), None, None),
        P(("layer", "rows"), None),
        P(("layer", "rows"), None),
        P(("layer", "rows"), None),
    )
    return jax.shard_map(
        local, mesh=mesh, in_specs=placed, out_specs=P("layer", "rows"), check_vma=False
    )
```

profile of v0, /device:TPU:11, one launch (start us, length us, event | category | flops | bytes accessed | tf_op | source)
XLA Modules:
  0.0 1182.1 jit_solution(7355832403112494992)
XLA Ops:
  6.5 0.0 all-gather.6.cloned.1.call-start
  6.5 0.7 all-gather.6.cloned.1.call-update
  7.3 26.5 %convert_element_type.9 = bf16[128,32,2880]{0,2,1:T(8,128)(2,1)} convert(f32[128,32,2880]{0,2,1:T(8,128)} %param.4) | non-fusion elementwise | flops 11796480 | bytes 70778880 | tf_op jit(solution)/shard_map/convert_element_type | solution.py:13
  33.7 32.0 %copy.11 = bf16[128,32,2880]{2,1,0:T(8,128)(2,1)} copy(bf16[128,32,2880]{0,2,1:T(8,128)(2,1)} %convert_element_type.9) | data formatting | bytes 47185920 | tf_op jit(solution)/shard_map/convert_element_type | solution.py:13
  65.7 36.3 %all-gather.6.cloned.1.call-done = bf16[16,180,2880]{2,1,0:T(8,128)(2,1)} async-done(((bf16[1,180,2880]{2,1,0:T(8,128)(2,1)}), bf16[16,180,2880]{2,1,0:T(8,128)(2,1)}) %all-gather.6.cloned.1.call-update) | async-done | bytes 16588816 | tf_op jit(solution)/shard_map/all_gather | solution.py:14
  102.0 17.0 %reshape.22 = bf16[2880,2880]{1,0:T(8,128)(2,1)} reshape(bf16[16,180,2880]{2,1,0:T(8,128)(2,1)} %all-gather.6.cloned.1.call-done) | data formatting | bytes 33177600
  118.9 119.8 %convolution_convert_fusion = bf16[4096,2880]{0,1:T(8,128)(2,1)} fusion(bf16[4096,2880]{1,0:T(8,128)(2,1)} %bitcast.20, bf16[2880,2880]{1,0:T(8,128)(2,1)} %reshape.22), kind=kOutput, calls=%fused_computation.1 | convolution fusion | flops 67959521280 | bytes 63774720 | tf_op jit(solution)/shard_map/dot_general | solution.py:15
  238.8 32.0 %copy.12 = bf16[4096,2880]{1,0:T(8,128)(2,1)} copy(bf16[4096,2880]{0,1:T(8,128)(2,1)} %convolution_convert_fusion) | data formatting | bytes 47185920 | tf_op jit(solution)/shard_map/convert_element_type | solution.py:16
  270.8 104.4 %reshape.18 = bf16[128,32,16,180]{3,2,1,0:T(8,128)(2,1)} reshape(bf16[4096,2880]{1,0:T(8,128)(2,1)} %copy.12) | data formatting | bytes 47185920 | tf_op jit(solution)/shard_map/reshape | solution.py:16
  375.2 96.2 %copy.13 = bf16[128,16,180,32]{0,3,2,1:T(8,128)(2,1)} copy(bf16[128,16,180,32]{2,1,3,0:T(8,128)(2,1)} %bitcast.18) | data formatting | bytes 47185920 | tf_op jit(solution)/shard_map/transpose | solution.py:17
  471.4 0.0 copy-start
  471.4 6.0 all-to-all-start
  477.4 0.0 all-gather.4.cloned.1.call-start
  477.4 0.7 all-gather.4.cloned.1.call-update
  478.1 0.0 copy-done
  478.1 0.3 add_bitcast_fusion
  478.5 557.6 %all-to-all-done = bf16[128,16,5760]{0,2,1:T(8,128)(2,1)} async-done(((bf16[128,16,5760]{0,2,1:T(8,128)(2,1)}), bf16[128,16,5760]{0,2,1:T(8,128)(2,1)}, u32[]{:S(2)}, u32[]{:S(2)}) %all-to-all-start) | async-done | bytes 23592992 | tf_op jit(solution)/shard_map/all_to_all | solution.py:18
  1036.1 30.6 %copy.14 = bf16[16,128,1,5760]{3,1,0,2:T(8,128)(2,1)} copy(bf16[16,128,1,5760]{1,3,0,2:T(8,128)(2,1)} %bitcast.5) | data formatting | bytes 47185920 | tf_op jit(solution)/shard_map/all_to_all | solution.py:18
  1066.8 0.0 all-gather.4.cloned.1.call-done
  1066.8 62.7 %bitcast_divide_fusion = f32[2048,5760]{0,1:T(8,128)} fusion(bf16[2048,5760]{1,0:T(8,128)(2,1)} %bitcast.21, bf16[2048,2048]{1,0:T(8,128)(2,1)} %all-gather.4.cloned.1.call-done, f32[2048,180]{0,1:T(8,128)S(1)} %add_bitcast_fusion), kind=kOutput, calls=%fused_computation | convolution fusion | flops 48330178560 | bytes 80642048 | tf_op jit(solution)/shard_map/dot_general | solution.py:21
  1129.5 45.8 %copy.15 = f32[2048,5760]{1,0:T(8,128)} copy(f32[2048,5760]{0,1:T(8,128)} %bitcast_divide_fusion) | data formatting | bytes 94371840 | tf_op jit(solution)/shard_map/div | solution.py:29
Async XLA Ops:
  6.5 95.4 %all-gather.6.cloned.1.call-start = ((), (), s32[]{:S(2)}) async-start(), calls=%async_computation.2 | async-start | bytes 18417664 | tf_op jit(solution)/shard_map/all_gather | solution.py:14
  471.4 6.7 copy-start
  471.4 564.7 %all-to-all-start = ((bf16[128,16,5760]{0,2,1:T(8,128)(2,1)}), bf16[128,16,5760]{0,2,1:T(8,128)(2,1)}, u32[]{:S(2)}, u32[]{:S(2)}) async-start(bf16[128,16,5760]{0,2,1:T(8,128)(2,1)} %bitcast.19), calls=%async_computation | async-start | bytes 47185920 | tf_op jit(solution)/shard_map/all_to_all | solution.py:18
  477.4 589.4 %all-gather.4.cloned.1.call-start = ((), (), s32[]{:S(2)}) async-start(), calls=%async_computation.1 | async-start | bytes 8912896 | tf_op jit(solution)/shard_map/all_gather | solution.py:22
Sparse Core Ops, SparseCore 0:
  8.9 92.9 all-gather.5
  480.3 292.9 all-gather.3
where the time goes:
time: 1190 us; the launch traced here: 1180 us
  waiting for transfers between devices  595 us (50%)
  local copies, waits for them, and re-layouts  358 us (30%)
  matrix products  183 us (15%)
  other arithmetic  26.8 us (2%)
  between operations  13.4 us (1%)
    all_to_all x1, waiting for transfers between devices, local(): lax.all_to_all(rotated, 'rows', split_axis=1, concat_axis=0, tiled=True)  558 us
    dot_general x1, matrix products, local(): rotated = jnp.dot(grad_low, full_in, preferred_element_type=jnp.float32)  120 us
    reshape x1, local copies, waits for them, and re-layouts, local(): rotated.astype(jnp.bfloat16).reshape(local_rows, grads, devices, span)  104 us
    transpose x1, local copies, waits for them, and re-layouts, local(): rotated.transpose(0, 2, 3, 1).reshape(local_rows, devices, span * grads)  96.2 us
    dot_general x1, matrix products, local(): lax.dot_general(lax.all_gather(out_basis, 'rows', axis=0, tiled=True), mo...  62.7 us
    div x1, local copies, waits for them, and re-layouts, local(): result = both.reshape(width_out, span, grads) / denom[:, :, None]  45.8 us
    all_gather x1, waiting for transfers between devices, local(): full_in = lax.all_gather(in_basis, 'rows', axis=0, tiled=True)  36.3 us
    convert_element_type x1, local copies, waits for them, and re-layouts, local(): rotated.astype(jnp.bfloat16).reshape(local_rows, grads, devices, span)  32 us
  transfers between devices with their start and end apart: 3, of which 2 were waited for; matrix products, arithmetic and copies ran while one was open for 8% of the time, Pallas kernels for 0%

commit v1 on v0

--- a/solution.py
+++ b/solution.py
@@ -1,10 +1,170 @@
+import functools
+
 import jax
 import jax.numpy as jnp
 from jax import lax
+from jax.experimental import pallas as pl
+from jax.experimental.pallas import tpu as pltpu
 from jax.sharding import PartitionSpec as P
 
-
-def local(gradients, in_basis, out_basis, eigen_seeds):
+LANES = 128
+WEIGHTS = (2, 4, 6, 7, 7, 7, 6, 4, 2)
+VMEM = 60 * 1024 * 1024
+
+
+def chunk_units(units):
+    total = sum(WEIGHTS)
+    edges = [round(sum(WEIGHTS[:n]) * units / total) for n in range(len(WEIGHTS) + 1)]
+    return [high - low for low, high in zip(edges, edges[1:]) if high > low]
+
+
+def rotate_kernel(grads, first, *refs):
+    if first:
+        basis_ref, grad_ref, out_ref, low_ref, basis_t, rows = refs
+    else:
+        basis_ref, grad_ref, out_ref, basis_t, rows = refs
+    step = pl.program_id(0)
+    columns = basis_ref.shape[1]
+
+    @pl.when(step == 0)
+    def _():
+        basis_t[...] = basis_ref[...].T
+
+    if first:
+        low_ref[0, :, :LANES] = grad_ref[0].astype(jnp.bfloat16)
+        low_ref[0, :, LANES:] = grad_ref[1].astype(jnp.bfloat16)
+        pair = low_ref[0]
+    else:
+        pair = grad_ref[0]
+    product = jnp.dot(basis_t[...], pair, preferred_element_type=jnp.float32)
+    for half in range(2):
+        rows[pl.ds(2 * step + half, columns, stride=grads), :] = product[:, half * LANES : (half + 1) * LANES]
+
+    @pl.when(step == pl.num_programs(0) - 1)
+    def _():
+        height = out_ref.shape[1]
+
+        def flush(owner, carry):
+            out_ref[owner] = rows[pl.ds(pl.multiple_of(owner * height, LANES), height), :].astype(jnp.bfloat16)
+            return carry
+
+        lax.fori_loop(0, out_ref.shape[0], flush, 0)
+
+
+def rotate(basis, grad, devices, grads, first):
+    depth, columns = basis.shape
+    height = columns // devices * grads
+    pairs = grads // 2
+    out_shape = [jax.ShapeDtypeStruct((devices, height, LANES), jnp.bfloat16)]
+    out_specs = [pl.BlockSpec((devices, height, LANES), lambda step: (0, 0, 0))]
+    if first:
+        grad_spec = pl.BlockSpec((2, depth, LANES), lambda step: (step, 0, 0))
+        out_shape.append(jax.ShapeDtypeStruct((pairs, depth, 2 * LANES), jnp.bfloat16))
+        out_specs.append(pl.BlockSpec((1, depth, 2 * LANES), lambda step: (step, 0, 0)))
+    else:
+        grad_spec = pl.BlockSpec((1, depth, 2 * LANES), lambda step: (step, 0, 0))
+    return pl.pallas_call(
+        functools.partial(rotate_kernel, grads, first),
+        grid=(pairs,),
+        in_specs=[pl.BlockSpec((depth, columns), lambda step: (0, 0)), grad_spec],
+        out_specs=out_specs,
+        out_shape=out_shape,
+        scratch_shapes=[
+            pltpu.VMEM((columns, depth), jnp.bfloat16),
+            pltpu.VMEM((columns * grads, LANES), jnp.float32),
+        ],
+        compiler_params=pltpu.CompilerParams(vmem_limit_bytes=VMEM),
+        cost_estimate=pl.CostEstimate(
+            flops=2 * columns * depth * grads * LANES,
+            bytes_accessed=2 * grads * depth * LANES * (3 if first else 1) + 2 * columns * (depth + grads * LANES),
+            transcendentals=0,
+        ),
+    )(basis, grad)
+
+
+def finish_kernel(begin, grads, *refs):
+    basis_ref, moved_ref, scale_ref, out_ref = refs[0], refs[1], refs[2], refs[-1]
+    devices = moved_ref.shape[0]
+    moved = jnp.concatenate([moved_ref[source] for source in range(devices)], axis=1)
+    both = lax.dot_general(basis_ref[...], moved, (((1,), (1,)), ((), ())), preferred_element_type=jnp.float32)
+    per_block = LANES // grads
+    height = both.shape[0]
+    lane = lax.broadcasted_iota(jnp.int32, (height, LANES), 1) // grads
+    for block in range(both.shape[1] // LANES):
+        where = begin + block * per_block
+        tile = scale_ref[:, where // LANES * LANES : (where // LANES + 1) * LANES]
+        scale = jnp.take_along_axis(tile, lane + where % LANES, axis=1)
+        part = slice(block * LANES, (block + 1) * LANES)
+        out_ref[:, part] = both[:, part] * scale
+
+
+def finish(basis_t, moved, scale, result, begin, span, grads):
+    devices, height, _ = moved.shape
+    width_out = basis_t.shape[0]
+    tile = width_out // 4
+    first_block = begin * grads // LANES
+    aliased = [] if result is None else [result]
+    return pl.pallas_call(
+        functools.partial(finish_kernel, begin, grads),
+        grid=(width_out // tile,),
+        in_specs=[
+            pl.BlockSpec((tile, basis_t.shape[1]), lambda row: (row, 0)),
+            pl.BlockSpec(moved.shape, lambda row: (0, 0, 0)),
+            pl.BlockSpec((tile, scale.shape[1]), lambda row: (row, 0)),
+        ]
+        + [pl.BlockSpec(memory_space=pl.ANY)] * len(aliased),
+        out_specs=pl.BlockSpec((pl.Element(tile), pl.Element(height)), lambda row: (row * tile, first_block * LANES)),
+        out_shape=jax.ShapeDtypeStruct((width_out, span * grads), jnp.float32),
+        input_output_aliases={3: 0} if aliased else {},
+        compiler_params=pltpu.CompilerParams(vmem_limit_bytes=VMEM),
+        cost_estimate=pl.CostEstimate(
+            flops=2 * width_out * height * basis_t.shape[1],
+            bytes_accessed=2 * basis_t.size + 2 * moved.size + 4 * width_out * height,
+            transcendentals=0,
+        ),
+    )(basis_t, moved, scale, *aliased)
+
+
+def pipelined(gradients, in_basis, out_basis, eigen_seeds):
+    devices = lax.axis_size("rows")
+    local_rows, grads, width_in = gradients.shape
+    span = width_in // devices
+    step = LANES // grads
+    counts = [step * n for n in chunk_units(span // step)]
+    begins = [sum(counts[:n]) for n in range(len(counts))]
+
+    def columns_of(begin, count):
+        return [in_basis[:, owner * span + begin : owner * span + begin + count] for owner in range(devices)]
+
+    def gathered(blocks):
+        return lax.all_gather(blocks, "rows", axis=0, tiled=True)
+
+    first_basis = gathered(jnp.concatenate(columns_of(0, counts[0]), axis=1))
+    rest = [piece for begin, count in zip(begins[1:], counts[1:]) for piece in columns_of(begin, count)]
+    rest_basis = gathered(jnp.concatenate(rest, axis=1))
+    basis_t = gathered(out_basis).T
+    denom = jnp.exp2(eigen_seeds.astype(jnp.float32) * 0.125 - 4.0) + 0.1
+    scale = jnp.pad((1.0 / denom).T, ((0, 0), (0, -span % LANES)))
+
+    grad = gradients.transpose(1, 2, 0)
+    moved = []
+    offset = 0
+    low = None
+    for n, count in enumerate(counts):
+        if n == 0:
+            rotated, low = rotate(first_basis, grad, devices, grads, True)
+        else:
+            basis = rest_basis[:, offset : offset + devices * count]
+            offset += devices * count
+            (rotated,) = rotate(basis, low, devices, grads, False)
+        moved.append(lax.all_to_all(rotated, "rows", split_axis=0, concat_axis=0, tiled=True))
+    result = None
+    for n, begin in enumerate(begins):
+        result = finish(basis_t, moved[n], scale, result, begin, span, grads)
+    return result
+
+
+def general(gradients, in_basis, out_basis, eigen_seeds):
     devices = lax.axis_size("rows")
     local_rows = gradients.shape[0]
     grads = gradients.shape[1]
@@ -30,6 +190,14 @@
     return result.reshape(width_out, span * grads)
 
 
+def local(gradients, in_basis, out_basis, eigen_seeds):
+    devices = lax.axis_size("rows")
+    local_rows, grads, width_in = gradients.shape
+    span = width_in // devices
+    fits = local_rows == LANES and LANES % grads == 0 and grads % 16 == 0 and span * grads % LANES == 0
+    return (pipelined if fits else general)(gradients, in_basis, out_basis, eigen_seeds)
+
+
 def solution(mesh):
     placed = (
         P(("layer", "rows"), None, None),

time: 1190 us -> 863 us (0.73)
  Pallas kernels: 0 us -> 311 us
  local copies, waits for them, and re-layouts: 358 us -> 73.3 us
  waiting for transfers between devices: 595 us -> 384 us
  matrix products: 183 us -> 0 us
  starting transfers between devices: 6.01 us -> 54.7 us
  other arithmetic: 26.8 us -> 0.56 us
  blocking collectives: 0 us -> 19.7 us
    pallas_call x0 -> x18, Pallas kernels: none -> 311 us  [the longest x9 213 us: rotate(): pl.pallas_call(functools.partial(rotate_kernel, grads, first), grid=(pair...]
    all_to_all x1 -> x9, waiting for transfers between devices: 558 us -> 305 us  [pipelined(): lax.all_to_all(rotated, 'rows', split_axis=0, concat_axis=0, tiled=True)]
    dot_general x2 -> x0, matrix products: 183 us -> none  [the longest x1 120 us: local(): rotated = jnp.dot(grad_low, full_in, preferred_element_type=jnp.float32)]
    reshape x1 -> x0, local copies, waits for them, and re-layouts: 104 us -> none  [local(): rotated.astype(jnp.bfloat16).reshape(local_rows, grads, devices, span)]
    transpose x1 -> x0, local copies, waits for them, and re-layouts: 96.2 us -> none  [local(): rotated.transpose(0, 2, 3, 1).reshape(local_rows, devices, span * grads)]
    convert_element_type x2 -> x0, local copies, waits for them, and re-layouts: 64 us -> none  [the longest x1 32 us: local(): rotated.astype(jnp.bfloat16).reshape(local_rows, grads, devices, span)]
    all_to_all x1 -> x9, starting transfers between devices: 5.97 us -> 54.7 us  [pipelined(): lax.all_to_all(rotated, 'rows', split_axis=0, concat_axis=0, tiled=True)]
    div x1 -> x0, local copies, waits for them, and re-layouts: 45.8 us -> none  [local(): result = both.reshape(width_out, span, grads) / denom[:, :, None]]
  transfers between devices with their start and end apart: 3 -> 11, of which waited for: 2 -> 8; matrix products, arithmetic and copies ran while one was open for 8% -> 5% of each run, Pallas kernels for 0% -> 35%
where the time goes in v1:
time: 863 us; the launch traced here: 857 us
  waiting for transfers between devices  384 us (44%)
  Pallas kernels  311 us (36%)
  local copies, waits for them, and re-layouts  73.3 us (8%)
  starting transfers between devices  54.7 us (6%)
  blocking collectives  19.7 us (2%)
  between operations  13.7 us (2%)
    all_to_all x9, waiting for transfers between devices, pipelined(): lax.all_to_all(rotated, 'rows', split_axis=0, concat_axis=0, tiled=True)  305 us
    pallas_call x9, Pallas kernels, rotate(): pl.pallas_call(functools.partial(rotate_kernel, grads, first), grid=(pair...  213 us
    pallas_call x9, Pallas kernels, finish(): pl.pallas_call(functools.partial(finish_kernel, begin, grads), grid=(widt...  97.8 us
    all_gather x2, waiting for transfers between devices, gathered(): return lax.all_gather(blocks, 'rows', axis=0, tiled=True)  79.5 us
    all_to_all x9, starting transfers between devices, pipelined(): lax.all_to_all(rotated, 'rows', split_axis=0, concat_axis=0, tiled=True)  54.7 us
    unnamed x50, local copies, waits for them, and re-layouts  26.8 us
    slice x4, local copies, waits for them, and re-layouts, pipelined(): basis = rest_basis[:, offset:offset + devices * count]  19.7 us
    all_gather x1, blocking collectives, gathered(): return lax.all_gather(blocks, 'rows', axis=0, tiled=True)  19.7 us
  transfers between devices with their start and end apart: 11, of which 8 were waited for; matrix products, arithmetic and copies ran while one was open for 5% of the time, Pallas kernels for 35%

profile of v1, /device:TPU:11, one launch (start us, length us, event | category | flops | bytes accessed | tf_op | source)
XLA Modules:
  0.0 857.4 jit_solution(11388252319471019134)
XLA Ops:
  17.2 14.6 %concatenate.6 = bf16[180,2752]{1,0:T(8,128)(2,1)} concatenate(bf16[180,16]{1,0:T(8,128)(2,1)} %get-tuple-element.159, bf16[180,16]{1,0:T(8,128)(2,1)} %get-tuple-element.158, bf16[180,16]{1,0:T(8,128)(2,1)} %get-tuple-element.157, bf16[180,16]{1,0:T(8,128)(2,1)} %get-tuple-element.156, bf16[180,16]{1,0:T(8,128)(2,1)} %get-tuple-element.155, bf16[180,16]{1,0:T(8,128)(2,1)} %get-tuple-element.154, ...), dimensions={1} | concatenate | bytes 1981440 | tf_op jit(solution)/shard_map/concatenate | solution.py:144
  32.2 19.7 %all-gather.1 = bf16[16,180,128]{2,1,0:T(8,128)(2,1)S(1)} all-gather(bf16[1,180,128]{2,1,0:T(8,128)(2,1)S(1)} %bitcast.17), channel_id=1, replica_groups=mesh['rows'=16,'layer'=2] {'rows'}, dimensions={0}, use_global_device_ids=true | all-gather | bytes 783360 | tf_op jit(solution)/shard_map/all_gather | solution.py:140
  53.0 30.6 %shard_map.46 = (bf16[16,256,128]{2,1,0:T(8,128)(2,1)}, bf16[16,2880,256]{2,1,0:T(8,128)(2,1)}) custom-call(bf16[2880,128]{1,0:T(8,128)(2,1)} %reshape.3.refs_0_, f32[32,2880,128]{2,1,0:T(8,128)} %bitcast.15), custom_call_target="tpu_custom_call" | custom-call | flops 3019898880 | bytes 72564736 | tf_op jit(solution)/shard_map/pallas_call | solution.py:66
  83.6 12.0 %all-to-all-start.8 = ((bf16[16,256,128]{2,1,0:T(8,128)(2,1)}), bf16[16,256,128]{2,1,0:T(8,128)(2,1)S(1)}, u32[]{:S(2)}, u32[]{:S(2)}) async-start(bf16[16,256,128]{2,1,0:T(8,128)(2,1)} %get-tuple-element.8), calls=%async_computation.8 | async-start | bytes 2097152 | tf_op jit(solution)/shard_map/all_to_all | solution.py:160
  95.6 79.5 %all-gather.7.cloned.1.call-done = bf16[16,180,2752]{2,1,0:T(8,128)(2,1)} async-done(((bf16[1,180,2752]{2,1,0:T(8,128)(2,1)}), bf16[16,180,2752]{2,1,0:T(8,128)(2,1)}) %all-gather.7.cloned.1.call-update) | async-done | bytes 15851536 | tf_op jit(solution)/shard_map/all_gather | solution.py:140
  175.1 16.4 %reshape.1 = bf16[2880,2752]{1,0:T(8,128)(2,1)} reshape(bf16[16,180,2752]{2,1,0:T(8,128)(2,1)} %all-gather.7.cloned.1.call-done) | data formatting | bytes 31703040
  196.0 20.7 %shard_map.54 = bf16[16,512,128]{2,1,0:T(8,128)(2,1)} custom-call(bf16[2880,256]{1,0:T(8,128)(2,1)} %get-tuple-element.9.refs_0_, bf16[16,2880,256]{2,1,0:T(8,128)(2,1)} %get-tuple-element.7.refs_1_), custom_call_target="tpu_custom_call" | custom-call | flops 6039797760 | bytes 27164672 | tf_op jit(solution)/shard_map/pallas_call | solution.py:66
  227.0 20.7 %shard_map.48 = bf16[16,512,128]{2,1,0:T(8,128)(2,1)} custom-call(bf16[2880,256]{1,0:T(8,128)(2,1)} %get-tuple-element.10.refs_0_, bf16[16,2880,256]{2,1,0:T(8,128)(2,1)} %get-tuple-element.7.refs_1_), custom_call_target="tpu_custom_call" | custom-call | flops 6039797760 | bytes 27164672 | tf_op jit(solution)/shard_map/pallas_call | solution.py:66
  247.7 26.7 %all-to-all-done.7.refs_1_ = bf16[16,512,128]{2,1,0:T(8,128)(2,1)S(1)} async-done(((bf16[16,512,128]{2,1,0:T(8,128)(2,1)}), bf16[16,512,128]{2,1,0:T(8,128)(2,1)S(1)}, u32[]{:S(2)}, u32[]{:S(2)}) %all-to-all-start.7) | async-done | bytes 2097184 | tf_op jit(solution)/shard_map/all_to_all | solution.py:160
  286.6 23.7 %shard_map.49 = bf16[16,768,128]{2,1,0:T(8,128)(2,1)} custom-call(bf16[2880,384]{1,0:T(8,128)(2,1)} %get-tuple-element.12.refs_0_, bf16[16,2880,256]{2,1,0:T(8,128)(2,1)} %get-tuple-element.7.refs_1_), custom_call_target="tpu_custom_call" | custom-call | flops 9059696640 | bytes 28950528 | tf_op jit(solution)/shard_map/pallas_call | solution.py:66
  310.3 17.6 %all-to-all-done.1.refs_1_ = bf16[16,512,128]{2,1,0:T(8,128)(2,1)S(1)} async-done(((bf16[16,512,128]{2,1,0:T(8,128)(2,1)}), bf16[16,512,128]{2,1,0:T(8,128)(2,1)S(1)}, u32[]{:S(2)}, u32[]{:S(2)}) %all-to-all-start.1) | async-done | bytes 2097184 | tf_op jit(solution)/shard_map/all_to_all | solution.py:160
  334.1 23.7 %shard_map.53 = bf16[16,768,128]{2,1,0:T(8,128)(2,1)} custom-call(bf16[2880,384]{1,0:T(8,128)(2,1)} %get-tuple-element.11.refs_0_, bf16[16,2880,256]{2,1,0:T(8,128)(2,1)} %get-tuple-element.7.refs_1_), custom_call_target="tpu_custom_call" | custom-call | flops 9059696640 | bytes 28950528 | tf_op jit(solution)/shard_map/pallas_call | solution.py:66
  357.8 46.2 %all-to-all-done.2.refs_1_ = bf16[16,768,128]{2,1,0:T(8,128)(2,1)S(1)} async-done(((bf16[16,768,128]{2,1,0:T(8,128)(2,1)}), bf16[16,768,128]{2,1,0:T(8,128)(2,1)S(1)}, u32[]{:S(2)}, u32[]{:S(2)}) %all-to-all-start.2) | async-done | bytes 3145760 | tf_op jit(solution)/shard_map/all_to_all | solution.py:160
  417.1 25.4 %shard_map.52 = bf16[16,896,128]{2,1,0:T(8,128)(2,1)} custom-call(bf16[2880,448]{1,0:T(8,128)(2,1)} %get-tuple-element.13.refs_0_, bf16[16,2880,256]{2,1,0:T(8,128)(2,1)} %get-tuple-element.7.refs_1_), custom_call_target="tpu_custom_call" | custom-call | flops 10569646080 | bytes 29843456 | tf_op jit(solution)/shard_map/pallas_call | solution.py:66
  442.5 38.0 %all-to-all-done.6.refs_1_ = bf16[16,768,128]{2,1,0:T(8,128)(2,1)} async-done(((bf16[16,768,128]{2,1,0:T(8,128)(2,1)}), bf16[16,768,128]{2,1,0:T(8,128)(2,1)}, u32[]{:S(2)}, u32[]{:S(2)}) %all-to-all-start.6) | async-done | bytes 3145760 | tf_op jit(solution)/shard_map/all_to_all | solution.py:160
  486.4 25.5 %shard_map.51 = bf16[16,896,128]{2,1,0:T(8,128)(2,1)} custom-call(bf16[2880,448]{1,0:T(8,128)(2,1)} %get-tuple-element.14.refs_0_, bf16[16,2880,256]{2,1,0:T(8,128)(2,1)} %get-tuple-element.7.refs_1_), custom_call_target="tpu_custom_call" | custom-call | flops 10569646080 | bytes 29843456 | tf_op jit(solution)/shard_map/pallas_call | solution.py:66
  511.9 105.2 %all-to-all-done.5.refs_1_ = bf16[16,896,128]{2,1,0:T(8,128)(2,1)} async-done(((bf16[16,896,128]{2,1,0:T(8,128)(2,1)}), bf16[16,896,128]{2,1,0:T(8,128)(2,1)}, u32[]{:S(2)}, u32[]{:S(2)}) %all-to-all-start.5) | async-done | bytes 3670048 | tf_op jit(solution)/shard_map/all_to_all | solution.py:160
  621.9 25.4 %shard_map.50 = bf16[16,896,128]{2,1,0:T(8,128)(2,1)} custom-call(bf16[2880,448]{1,0:T(8,128)(2,1)} %get-tuple-element.15.refs_0_, bf16[16,2880,256]{2,1,0:T(8,128)(2,1)} %get-tuple-element.7.refs_1_), custom_call_target="tpu_custom_call" | custom-call | flops 10569646080 | bytes 29843456 | tf_op jit(solution)/shard_map/pallas_call | solution.py:66
  647.3 55.8 %all-to-all-done.4.refs_1_ = bf16[16,896,128]{2,1,0:T(8,128)(2,1)} async-done(((bf16[16,896,128]{2,1,0:T(8,128)(2,1)}), bf16[16,896,128]{2,1,0:T(8,128)(2,1)}, u32[]{:S(2)}, u32[]{:S(2)}) %all-to-all-start.4) | async-done | bytes 3670048 | tf_op jit(solution)/shard_map/all_to_all | solution.py:160
  721.5 17.4 %shard_map.47 = bf16[16,256,128]{2,1,0:T(8,128)(2,1)} custom-call(bf16[2880,128]{1,0:T(8,128)(2,1)} %slice.608.refs_0_, bf16[16,2880,256]{2,1,0:T(8,128)(2,1)} %get-tuple-element.7.refs_1_), custom_call_target="tpu_custom_call" | custom-call | flops 3019898880 | bytes 25378816 | tf_op jit(solution)/shard_map/pallas_call | solution.py:66
  760.2 13.6 %shard_map.58.refs_3_ = f32[2048,5760]{1,0:T(8,128)} custom-call(bf16[2048,2048]{1,0:T(8,128)(2,1)} %bitcast.9, bf16[16,896,128]{2,1,0:T(8,128)(2,1)} %all-to-all-done.5.refs_1_, f32[2048,256]{1,0:T(8,128)} %pad.4.refs_2_, f32[2048,5760]{1,0:T(8,128)} %shard_map.57.refs_3_), custom_call_target="tpu_custom_call", output_to_operand_aliasing={{}: (3, {})} | custom-call | flops 7516192768 | bytes 19398656 | tf_op jit(solution)/shard_map/pallas_call | solution.py:107
  773.8 15.3 %all-to-all-done.3.refs_1_ = bf16[16,896,128]{2,1,0:T(8,128)(2,1)} async-done(((bf16[16,896,128]{2,1,0:T(8,128)(2,1)}), bf16[16,896,128]{2,1,0:T(8,128)(2,1)}, u32[]{:S(2)}, u32[]{:S(2)}) %all-to-all-start.3) | async-done | bytes 3670048 | tf_op jit(solution)/shard_map/all_to_all | solution.py:160
  793.9 13.6 %shard_map.59.refs_3_ = f32[2048,5760]{1,0:T(8,128)} custom-call(bf16[2048,2048]{1,0:T(8,128)(2,1)} %bitcast.10, bf16[16,896,128]{2,1,0:T(8,128)(2,1)} %all-to-all-done.4.refs_1_, f32[2048,256]{1,0:T(8,128)} %pad.4.refs_2_, f32[2048,5760]{1,0:T(8,128)} %shard_map.58.refs_3_), custom_call_target="tpu_custom_call", output_to_operand_aliasing={{}: (3, {})} | custom-call | flops 7516192768 | bytes 19398656 | tf_op jit(solution)/shard_map/pallas_call | solution.py:107
  807.5 13.6 %shard_map.60.refs_3_ = f32[2048,5760]{1,0:T(8,128)} custom-call(bf16[2048,2048]{1,0:T(8,128)(2,1)} %bitcast.11, bf16[16,896,128]{2,1,0:T(8,128)(2,1)} %all-to-all-done.3.refs_1_, f32[2048,256]{1,0:T(8,128)} %pad.4.refs_2_, f32[2048,5760]{1,0:T(8,128)} %shard_map.59.refs_3_), custom_call_target="tpu_custom_call", output_to_operand_aliasing={{}: (3, {})} | custom-call | flops 7516192768 | bytes 19398656 | tf_op jit(solution)/shard_map/pallas_call | solution.py:107
  (86 shorter events, 142.6 us)
Async XLA Ops:
  6.5 168.5 %all-gather.7.cloned.1.call-start = ((), (), s32[]{:S(2)}) async-start(), calls=%async_computation.10 | async-start | bytes 17616896 | tf_op jit(solution)/shard_map/all_gather | solution.py:140
  17.0 14.8 %copy-start.9 = (bf16[180,8]{1,0:T(8,128)(2,1)S(1)}, bf16[180,8]{1,0:T(8,128)(2,1)}, u32[]{:S(2)}) copy-start(bf16[180,8]{1,0:T(8,128)(2,1)} %get-tuple-element.32) | copy-start | bytes 8644
  17.1 14.8 %copy-start.10 = (bf16[180,8]{1,0:T(8,128)(2,1)S(1)}, bf16[180,8]{1,0:T(8,128)(2,1)}, u32[]{:S(2)}) copy-start(bf16[180,8]{1,0:T(8,128)(2,1)} %get-tuple-element.33) | copy-start | bytes 8644
  17.1 14.8 %copy-start.11 = (bf16[180,8]{1,0:T(8,128)(2,1)S(1)}, bf16[180,8]{1,0:T(8,128)(2,1)}, u32[]{:S(2)}) copy-start(bf16[180,8]{1,0:T(8,128)(2,1)} %get-tuple-element.34) | copy-start | bytes 8644
  17.1 14.8 %copy-start.12 = (bf16[180,8]{1,0:T(8,128)(2,1)S(1)}, bf16[180,8]{1,0:T(8,128)(2,1)}, u32[]{:S(2)}) copy-start(bf16[180,8]{1,0:T(8,128)(2,1)} %get-tuple-element.35) | copy-start | bytes 8644
  17.1 14.8 %copy-start.13 = (bf16[180,8]{1,0:T(8,128)(2,1)S(1)}, bf16[180,8]{1,0:T(8,128)(2,1)}, u32[]{:S(2)}) copy-start(bf16[180,8]{1,0:T(8,128)(2,1)} %get-tuple-element.36) | copy-start | bytes 8644
  17.1 14.8 %copy-start.14 = (bf16[180,8]{1,0:T(8,128)(2,1)S(1)}, bf16[180,8]{1,0:T(8,128)(2,1)}, u32[]{:S(2)}) copy-start(bf16[180,8]{1,0:T(8,128)(2,1)} %get-tuple-element.37) | copy-start | bytes 8644
  17.1 14.8 %copy-start.15 = (bf16[180,8]{1,0:T(8,128)(2,1)S(1)}, bf16[180,8]{1,0:T(8,128)(2,1)}, u32[]{:S(2)}) copy-start(bf16[180,8]{1,0:T(8,128)(2,1)} %get-tuple-element.38) | copy-start | bytes 8644
  17.1 14.8 %copy-start.16 = (bf16[180,8]{1,0:T(8,128)(2,1)S(1)}, bf16[180,8]{1,0:T(8,128)(2,1)}, u32[]{:S(2)}) copy-start(bf16[180,8]{1,0:T(8,128)(2,1)} %get-tuple-element.39) | copy-start | bytes 8644
  17.1 14.8 %copy-start.17 = (bf16[180,8]{1,0:T(8,128)(2,1)S(1)}, bf16[180,8]{1,0:T(8,128)(2,1)}, u32[]{:S(2)}) copy-start(bf16[180,8]{1,0:T(8,128)(2,1)} %get-tuple-element.40) | copy-start | bytes 8644
  17.1 14.8 %copy-start.18 = (bf16[180,8]{1,0:T(8,128)(2,1)S(1)}, bf16[180,8]{1,0:T(8,128)(2,1)}, u32[]{:S(2)}) copy-start(bf16[180,8]{1,0:T(8,128)(2,1)} %get-tuple-element.41) | copy-start | bytes 8644
  17.1 14.8 %copy-start.19 = (bf16[180,8]{1,0:T(8,128)(2,1)S(1)}, bf16[180,8]{1,0:T(8,128)(2,1)}, u32[]{:S(2)}) copy-start(bf16[180,8]{1,0:T(8,128)(2,1)} %get-tuple-element.42) | copy-start | bytes 8644
  17.2 14.8 %copy-start.20 = (bf16[180,8]{1,0:T(8,128)(2,1)S(1)}, bf16[180,8]{1,0:T(8,128)(2,1)}, u32[]{:S(2)}) copy-start(bf16[180,8]{1,0:T(8,128)(2,1)} %get-tuple-element.43) | copy-start | bytes 8644
  83.6 133.1 %all-to-all-start.8 = ((bf16[16,256,128]{2,1,0:T(8,128)(2,1)}), bf16[16,256,128]{2,1,0:T(8,128)(2,1)S(1)}, u32[]{:S(2)}, u32[]{:S(2)}) async-start(bf16[16,256,128]{2,1,0:T(8,128)(2,1)} %get-tuple-element.8), calls=%async_computation.8 | async-start | bytes 2097152 | tf_op jit(solution)/shard_map/all_to_all | solution.py:160
  217.7 56.7 %all-to-all-start.7 = ((bf16[16,512,128]{2,1,0:T(8,128)(2,1)}), bf16[16,512,128]{2,1,0:T(8,128)(2,1)S(1)}, u32[]{:S(2)}, u32[]{:S(2)}) async-start(bf16[16,512,128]{2,1,0:T(8,128)(2,1)} %shard_map.54), calls=%async_computation.7 | async-start | bytes 4194304 | tf_op jit(solution)/shard_map/all_to_all | solution.py:160
  275.8 52.2 %all-to-all-start.1 = ((bf16[16,512,128]{2,1,0:T(8,128)(2,1)}), bf16[16,512,128]{2,1,0:T(8,128)(2,1)S(1)}, u32[]{:S(2)}, u32[]{:S(2)}) async-start(bf16[16,512,128]{2,1,0:T(8,128)(2,1)} %shard_map.48), calls=%async_computation.1 | async-start | bytes 4194304 | tf_op jit(solution)/shard_map/all_to_all | solution.py:160
  329.3 74.7 %all-to-all-start.2 = ((bf16[16,768,128]{2,1,0:T(8,128)(2,1)}), bf16[16,768,128]{2,1,0:T(8,128)(2,1)S(1)}, u32[]{:S(2)}, u32[]{:S(2)}) async-start(bf16[16,768,128]{2,1,0:T(8,128)(2,1)} %shard_map.49), calls=%async_computation.2 | async-start | bytes 6291456 | tf_op jit(solution)/shard_map/all_to_all | solution.py:160
  405.7 74.8 %all-to-all-start.6 = ((bf16[16,768,128]{2,1,0:T(8,128)(2,1)}), bf16[16,768,128]{2,1,0:T(8,128)(2,1)}, u32[]{:S(2)}, u32[]{:S(2)}) async-start(bf16[16,768,128]{2,1,0:T(8,128)(2,1)} %shard_map.53), calls=%async_computation.6 | async-start | bytes 6291456 | tf_op jit(solution)/shard_map/all_to_all | solution.py:160
  442.5 42.9 %copy-start.6 = (bf16[128,2048]{1,0:T(8,128)(2,1)S(1)}, bf16[128,2048]{1,0:T(8,128)(2,1)}, u32[]{:S(2)}) copy-start(bf16[128,2048]{1,0:T(8,128)(2,1)} %param.6) | copy-start | bytes 1572868
  480.5 136.7 %all-to-all-start.5 = ((bf16[16,896,128]{2,1,0:T(8,128)(2,1)}), bf16[16,896,128]{2,1,0:T(8,128)(2,1)}, u32[]{:S(2)}, u32[]{:S(2)}) async-start(bf16[16,896,128]{2,1,0:T(8,128)(2,1)} %shard_map.52), calls=%async_computation.5 | async-start | bytes 7340032 | tf_op jit(solution)/shard_map/all_to_all | solution.py:160
  485.3 226.4 %all-gather.5.cloned.1.call-start = ((), (), s32[]{:S(2)}) async-start(), calls=%async_computation.9 | async-start | bytes 8912896 | tf_op jit(solution)/shard_map/all_gather | solution.py:140
  617.2 85.9 %all-to-all-start.4 = ((bf16[16,896,128]{2,1,0:T(8,128)(2,1)}), bf16[16,896,128]{2,1,0:T(8,128)(2,1)}, u32[]{:S(2)}, u32[]{:S(2)}) async-start(bf16[16,896,128]{2,1,0:T(8,128)(2,1)} %shard_map.51), calls=%async_computation.4 | async-start | bytes 7340032 | tf_op jit(solution)/shard_map/all_to_all | solution.py:160
  703.1 86.0 %all-to-all-start.3 = ((bf16[16,896,128]{2,1,0:T(8,128)(2,1)}), bf16[16,896,128]{2,1,0:T(8,128)(2,1)}, u32[]{:S(2)}, u32[]{:S(2)}) async-start(bf16[16,896,128]{2,1,0:T(8,128)(2,1)} %shard_map.50), calls=%async_computation.3 | async-start | bytes 7340032 | tf_op jit(solution)/shard_map/all_to_all | solution.py:160
  789.1 53.3 %all-to-all-start = ((bf16[16,256,128]{2,1,0:T(8,128)(2,1)}), bf16[16,256,128]{2,1,0:T(8,128)(2,1)S(1)}, u32[]{:S(2)}, u32[]{:S(2)}) async-start(bf16[16,256,128]{2,1,0:T(8,128)(2,1)} %shard_map.47), calls=%async_computation | async-start | bytes 2097152 | tf_op jit(solution)/shard_map/all_to_all | solution.py:160
  (10 other events, 69.7 us)
Sparse Core Ops, SparseCore 0:
  31.9 143.1 all-gather.6
  488.3 127.8 all-gather.4

commit v2 on v0

--- a/solution.py
+++ b/solution.py
@@ -1,10 +1,223 @@
+import functools
+
 import jax
 import jax.numpy as jnp
 from jax import lax
+from jax.experimental import pallas as pl
+from jax.experimental.pallas import tpu as pltpu
 from jax.sharding import PartitionSpec as P
 
 
-def local(gradients, in_basis, out_basis, eigen_seeds):
+LANES = 128
+WEIGHTS = (4, 8, 10, 10, 6, 4, 3)
+GROUPS = (0, 1, 2)
+VMEM = 60 * 1024 * 1024
+
+
+def chunk_units(units):
+    total = sum(WEIGHTS)
+    edges = [round(sum(WEIGHTS[:n]) * units / total) for n in range(len(WEIGHTS) + 1)]
+    return [high - low for low, high in zip(edges, edges[1:]) if high > low]
+
+
+def full_tiles(columns):
+    return -(-columns // LANES) * LANES
+
+
+def exchange(block, flip):
+    devices = lax.axis_size("rows")
+    return lax.ppermute(block, "rows", [(source, source ^ flip) for source in range(devices)])
+
+
+def far_bits(devices):
+    return [1 << bit for bit in reversed(range(devices.bit_length() - 1))]
+
+
+def offsets(devices):
+    order = [0]
+    for bit in far_bits(devices):
+        order = order + [bit | other for other in order]
+    return order
+
+
+def gather_absolute(block):
+    me = lax.axis_index("rows")
+    for bit in far_bits(lax.axis_size("rows")):
+        other = exchange(block, bit)
+        low = (me & bit) == 0
+        block = jnp.concatenate([jnp.where(low, block, other), jnp.where(low, other, block)])
+    return block
+
+
+def arrange_kernel(devices, spans, basis_ref, *outs):
+    span = basis_ref.shape[1] // devices
+    whole = basis_ref[...].astype(jnp.float32)
+    for out_ref, group in zip(outs, spans):
+        pieces = []
+        for begin, count in group:
+            pieces += [whole[:, owner * span + begin : owner * span + begin + count] for owner in range(devices)]
+        blank = out_ref.shape[2] - sum(piece.shape[1] for piece in pieces)
+        if blank:
+            pieces.append(jnp.zeros((whole.shape[0], blank), jnp.float32))
+        out_ref[0] = jnp.concatenate(pieces, axis=1).astype(jnp.bfloat16)
+
+
+def arrange(in_basis, devices, spans):
+    rows, _ = in_basis.shape
+    return pl.pallas_call(
+        functools.partial(arrange_kernel, devices, spans),
+        out_shape=[
+            jax.ShapeDtypeStruct((1, rows, full_tiles(devices * sum(count for _, count in group))), jnp.bfloat16)
+            for group in spans
+        ],
+        compiler_params=pltpu.CompilerParams(vmem_limit_bytes=VMEM),
+    )(in_basis)
+
+
+def rotate_kernel(columns, grads, sources, order, me_ref, *refs):
+    basis_ref, grad_ref = refs[:2]
+    outs = refs[2 : 2 + len(order)]
+    stage, basis_t, rows, pair = refs[-4:]
+    step = pl.program_id(0)
+    part = basis_ref.shape[1]
+
+    @pl.when(step == 0)
+    def _():
+        for slot, source in enumerate(sources):
+            stage[source * part : (source + 1) * part, :] = basis_ref[slot].astype(jnp.float32)
+        basis_t[...] = stage[...].T.astype(jnp.bfloat16)
+
+    pair[:, :LANES] = grad_ref[0].astype(jnp.bfloat16)
+    pair[:, LANES:] = grad_ref[1].astype(jnp.bfloat16)
+    product = jnp.dot(basis_t[:columns, :], pair[...], preferred_element_type=jnp.float32)
+    for half in range(2):
+        rows[pl.ds(2 * step + half, columns, stride=grads), :] = product[:, half * LANES : (half + 1) * LANES]
+
+    @pl.when(step == pl.num_programs(0) - 1)
+    def _():
+        height = outs[0].shape[0]
+        for out_ref, offset in zip(outs, order):
+            owner = me_ref[0] ^ offset
+            out_ref[...] = rows[pl.ds(pl.multiple_of(owner * height, LANES), height), :].astype(jnp.bfloat16)
+
+
+def rotate(me, basis, begin, columns, grad, grads, sources, order):
+    devices, part, _ = basis.shape
+    depth = devices * part
+    height = columns // devices * grads
+    wide = full_tiles(columns)
+    basis_spec = pl.BlockSpec(
+        (pl.Element(devices), pl.Element(part), pl.Element(wide)), lambda step, me: (0, 0, begin)
+    )
+    return pl.pallas_call(
+        functools.partial(rotate_kernel, columns, grads, sources, order),
+        grid_spec=pltpu.PrefetchScalarGridSpec(
+            num_scalar_prefetch=1,
+            grid=(grads // 2,),
+            in_specs=[basis_spec, pl.BlockSpec((2, depth, LANES), lambda step, me: (step, 0, 0))],
+            out_specs=[pl.BlockSpec((height, LANES), lambda step, me: (0, 0))] * devices,
+            scratch_shapes=[
+                pltpu.VMEM((depth, wide), jnp.float32),
+                pltpu.VMEM((wide, depth), jnp.bfloat16),
+                pltpu.VMEM((columns * grads, LANES), jnp.float32),
+                pltpu.VMEM((depth, 2 * LANES), jnp.bfloat16),
+            ],
+        ),
+        out_shape=[jax.ShapeDtypeStruct((height, LANES), jnp.bfloat16)] * devices,
+        compiler_params=pltpu.CompilerParams(vmem_limit_bytes=VMEM),
+        cost_estimate=pl.CostEstimate(
+            flops=2 * columns * depth * grads * LANES,
+            bytes_accessed=4 * grads * depth * LANES + 2 * columns * (depth + grads * LANES),
+            transcendentals=0,
+        ),
+    )(me, basis, grad)
+
+
+def finish_kernel(begin, grads, devices, *refs):
+    basis_ref, scale_ref, out_ref = refs[0], refs[1], refs[-1]
+    moved = jnp.concatenate([ref[...] for ref in refs[2 : 2 + devices]], axis=1)
+    basis = jnp.concatenate([basis_ref[slot] for slot in range(devices)], axis=1)
+    both = lax.dot_general(basis, moved, (((1,), (1,)), ((), ())), preferred_element_type=jnp.float32)
+    per_block = LANES // grads
+    height = both.shape[0]
+    lane = lax.broadcasted_iota(jnp.int32, (height, LANES), 1) // grads
+    for block in range(both.shape[1] // LANES):
+        where = begin + block * per_block
+        tile = scale_ref[:, where // LANES * LANES : (where // LANES + 1) * LANES]
+        scale = jnp.take_along_axis(tile, lane + where % LANES, axis=1)
+        part = slice(block * LANES, (block + 1) * LANES)
+        out_ref[:, part] = both[:, part] * scale
+
+
+def finish(basis, scale, moved, result, begin, span, grads):
+    devices, width_out, _ = basis.shape
+    height, _ = moved[0].shape
+    tile = width_out // 4
+    aliased = [] if result is None else [result]
+    return pl.pallas_call(
+        functools.partial(finish_kernel, begin, grads, devices),
+        grid=(width_out // tile,),
+        in_specs=[
+            pl.BlockSpec((devices, tile, LANES), lambda row: (0, row, 0)),
+            pl.BlockSpec((tile, scale.shape[1]), lambda row: (row, 0)),
+        ]
+        + [pl.BlockSpec((height, LANES), lambda row: (0, 0))] * devices
+        + [pl.BlockSpec(memory_space=pl.ANY)] * len(aliased),
+        out_specs=pl.BlockSpec((pl.Element(tile), pl.Element(height)), lambda row: (row * tile, begin * grads)),
+        out_shape=jax.ShapeDtypeStruct((width_out, span * grads), jnp.float32),
+        input_output_aliases={2 + devices: 0} if aliased else {},
+        compiler_params=pltpu.CompilerParams(vmem_limit_bytes=VMEM),
+        cost_estimate=pl.CostEstimate(
+            flops=2 * width_out * height * devices * LANES,
+            bytes_accessed=2 * basis.size + 2 * devices * height * LANES + 4 * width_out * height,
+            transcendentals=0,
+        ),
+    )(basis, scale, *moved, *aliased)
+
+
+def pipelined(gradients, in_basis, out_basis, eigen_seeds):
+    devices = lax.axis_size("rows")
+    _, grads, width_in = gradients.shape
+    span = width_in // devices
+    step = LANES // grads
+    counts = [step * n for n in chunk_units(span // step)]
+    begins = [sum(counts[:n]) for n in range(len(counts))]
+    chunks = list(zip(begins, counts))
+    spans = [chunks[low:high] for low, high in zip(GROUPS, GROUPS[1:] + (len(chunks),))]
+    order = offsets(devices)
+    me = lax.axis_index("rows").astype(jnp.int32)[None]
+
+    (early,) = arrange(in_basis, devices, spans[:1])
+    gathered = [lax.all_gather(block, "rows", axis=0, tiled=True) for block in arrange(in_basis, devices, spans[1:])]
+    early = gather_absolute(early)
+    early, out_basis = lax.optimization_barrier((early, out_basis))
+    gathered = [early] + gathered
+    basis = out_basis.T[None]
+    denom = jnp.exp2(eigen_seeds.astype(jnp.float32) * 0.125 - 4.0) + 0.1
+    scale = jnp.pad((1.0 / denom).T, ((0, 0), (0, -span % LANES)))
+    for n, bit in enumerate(far_bits(devices)):
+        incoming = exchange(basis, bit)
+        basis = jnp.concatenate([basis, incoming])
+
+    grad = gradients.transpose(1, 2, 0)
+    far = sorted(range(devices), key=lambda slot: -order[slot])
+    moved = []
+    for n, (begin, count) in enumerate(chunks):
+        group = max(index for index, low in enumerate(GROUPS) if low <= n)
+        column = (begin - begins[GROUPS[group]]) * devices
+        sources = list(range(devices)) if group else order
+        rotated = rotate(me, gathered[group], column, count * devices, grad, grads, sources, order)
+        if n > 1:
+            rotated, moved[n - 2], grad = lax.optimization_barrier((rotated, moved[n - 2], grad))
+        arrived = {slot: exchange(rotated[slot], order[slot]) if order[slot] else rotated[slot] for slot in far}
+        moved.append([arrived[slot] for slot in range(devices)])
+    result = None
+    for n, begin in enumerate(begins):
+        result = finish(basis, scale, moved[n], result, begin, span, grads)
+    return result
+
+
+def general(gradients, in_basis, out_basis, eigen_seeds):
     devices = lax.axis_size("rows")
     local_rows = gradients.shape[0]
     grads = gradients.shape[1]
@@ -30,6 +243,15 @@
     return result.reshape(width_out, span * grads)
 
 
+def local(gradients, in_basis, out_basis, eigen_seeds):
+    devices = lax.axis_size("rows")
+    local_rows, grads, width_in = gradients.shape
+    span = width_in // devices
+    fits = local_rows == LANES and LANES % grads == 0 and grads % 16 == 0 and span * grads % LANES == 0
+    fits = fits and devices & (devices - 1) == 0
+    return (pipelined if fits else general)(gradients, in_basis, out_basis, eigen_seeds)
+
+
 def solution(mesh):
     placed = (
         P(("layer", "rows"), None, None),

time: 1190 us -> 885 us (0.74)
  local copies, waits for them, and re-layouts: 358 us -> 16.7 us
  Pallas kernels: 0 us -> 304 us
  waiting for transfers between devices: 595 us -> 328 us
  starting transfers between devices: 6.01 us -> 202 us
  matrix products: 183 us -> 0 us
  other arithmetic: 26.8 us -> 8.42 us
    all_to_all x1 -> x0, waiting for transfers between devices: 558 us -> none  [local(): lax.all_to_all(rotated, 'rows', split_axis=1, concat_axis=0, tiled=True)]
    ppermute x0 -> x113, waiting for transfers between devices: none -> 327 us  [exchange(): lax.ppermute(block, 'rows', [(source, source ^ flip) for source in range(...]
    pallas_call x0 -> x16, Pallas kernels: none -> 304 us  [the longest x7 211 us: rotate(): pl.pallas_call(functools.partial(rotate_kernel, columns, grads, sources,...]
    ppermute x0 -> x113, starting transfers between devices: none -> 202 us  [exchange(): lax.ppermute(block, 'rows', [(source, source ^ flip) for source in range(...]
    dot_general x2 -> x0, matrix products: 183 us -> none  [the longest x1 120 us: local(): rotated = jnp.dot(grad_low, full_in, preferred_element_type=jnp.float32)]
    reshape x1 -> x0, local copies, waits for them, and re-layouts: 104 us -> none  [local(): rotated.astype(jnp.bfloat16).reshape(local_rows, grads, devices, span)]
    transpose x1 -> x0, local copies, waits for them, and re-layouts: 96.2 us -> none  [local(): rotated.transpose(0, 2, 3, 1).reshape(local_rows, devices, span * grads)]
    convert_element_type x2 -> x0, local copies, waits for them, and re-layouts: 64 us -> none  [the longest x1 32 us: local(): rotated.astype(jnp.bfloat16).reshape(local_rows, grads, devices, span)]
  transfers between devices with their start and end apart: 3 -> 115, of which waited for: 2 -> 32; matrix products, arithmetic and copies ran while one was open for 8% -> 3% of each run, Pallas kernels for 0% -> 33%
where the time goes in v2:
time: 885 us; the launch traced here: 874 us
  waiting for transfers between devices  328 us (37%)
  Pallas kernels  304 us (34%)
  starting transfers between devices  202 us (23%)
  local copies, waits for them, and re-layouts  16.7 us (2%)
  between operations  15.1 us (2%)
    ppermute x113, waiting for transfers between devices, exchange(): lax.ppermute(block, 'rows', [(source, source ^ flip) for source in range(...  327 us
    pallas_call x7, Pallas kernels, rotate(): pl.pallas_call(functools.partial(rotate_kernel, columns, grads, sources,...  211 us
    ppermute x113, starting transfers between devices, exchange(): lax.ppermute(block, 'rows', [(source, source ^ flip) for source in range(...  202 us
    pallas_call x7, Pallas kernels, finish(): pl.pallas_call(functools.partial(finish_kernel, begin, grads, devices), g...  87.3 us
  transfers between devices with their start and end apart: 115, of which 32 were waited for; matrix products, arithmetic and copies ran while one was open for 3% of the time, Pallas kernels for 33%

profile of v2, /device:TPU:11, one launch (start us, length us, event | category | flops | bytes accessed | tf_op | source)
XLA Modules:
  0.0 874.4 jit_solution(2369274720953457929)
XLA Ops:
  53.5 23.0 %collective-permute-done.4 = bf16[1,2048,128]{2,1,0:T(8,128)(2,1)S(1)} collective-permute-done((bf16[1,2048,128]{2,1,0:T(8,128)(2,1)S(1)}, bf16[1,2048,128]{2,1,0:T(8,128)(2,1)S(1)}, u32[]{:S(2)}, u32[]{:S(2)}) %collective-permute-start.4) | collective-permute-done | bytes 524320 | tf_op jit(solution)/shard_map/ppermute | solution.py:29
  81.4 47.7 %collective-permute-done.5 = bf16[2,2048,128]{2,1,0:T(8,128)(2,1)S(1)} collective-permute-done((bf16[2,2048,128]{2,1,0:T(8,128)(2,1)S(1)}, bf16[2,2048,128]{2,1,0:T(8,128)(2,1)S(1)}, u32[]{:S(2)}, u32[]{:S(2)}) %collective-permute-start.5) | collective-permute-done | bytes 1048608 | tf_op jit(solution)/shard_map/ppermute | solution.py:29
  130.7 28.0 %shard_map.49 = (bf16[512,128]{1,0:T(8,128)(2,1)}, bf16[512,128]{1,0:T(8,128)(2,1)}, bf16[512,128]{1,0:T(8,128)(2,1)}, bf16[512,128]{1,0:T(8,128)(2,1)}, bf16[51...) custom-call(s32[1]{0:T(128)} %bitcast.4.me_ref, ...), custom_call_target="tpu_custom_call" | custom-call | flops 6039797760 | bytes 50757632 | tf_op jit(solution)/shard_map/pallas_call | solution.py:112
  181.0 41.4 %collective-permute-done.11.refs_6_ = bf16[512,128]{1,0:T(8,128)(2,1)} collective-permute-done((bf16[512,128]{1,0:T(8,128)(2,1)}, bf16[512,128]{1,0:T(8,128)(2,1)}, u32[]{:S(2)}, u32[]{:S(2)}) %collective-permute-start.11) | collective-permute-done | bytes 131104 | tf_op jit(solution)/shard_map/ppermute | solution.py:29
  228.5 32.3 %shard_map.51 = (bf16[1024,128]{1,0:T(8,128)(2,1)}, bf16[1024,128]{1,0:T(8,128)(2,1)}, bf16[1024,128]{1,0:T(8,128)(2,1)}, bf16[1024,128]{1,0:T(8,128)(2,1)}, bf1...) custom-call(s32[1]{0:T(128)} %bitcast.4.me_ref, ...), custom_call_target="tpu_custom_call" | custom-call | flops 12079595520 | bytes 54329344 | tf_op jit(solution)/shard_map/pallas_call | solution.py:112
  267.6 14.1 %collective-permute-done.20.refs_15_ = bf16[512,128]{1,0:T(8,128)(2,1)S(1)} collective-permute-done((bf16[512,128]{1,0:T(8,128)(2,1)S(1)}, bf16[512,128]{1,0:T(8,128)(2,1)S(1)}, u32[]{:S(2)}, u32[]{:S(2)}) %collective-permute-start.20) | collective-permute-done | bytes 131104 | tf_op jit(solution)/shard_map/ppermute | solution.py:29
  294.1 10.9 %collective-permute-done.25.refs_5_ = bf16[1024,128]{1,0:T(8,128)(2,1)} collective-permute-done((bf16[1024,128]{1,0:T(8,128)(2,1)}, bf16[1024,128]{1,0:T(8,128)(2,1)}, u32[]{:S(2)}, u32[]{:S(2)}) %collective-permute-start.25) | collective-permute-done | bytes 262176 | tf_op jit(solution)/shard_map/ppermute | solution.py:29
  308.0 13.9 %collective-permute-done.27.refs_7_ = bf16[1024,128]{1,0:T(8,128)(2,1)} collective-permute-done((bf16[1024,128]{1,0:T(8,128)(2,1)}, bf16[1024,128]{1,0:T(8,128)(2,1)}, u32[]{:S(2)}, u32[]{:S(2)}) %collective-permute-start.27) | collective-permute-done | bytes 262176 | tf_op jit(solution)/shard_map/ppermute | solution.py:29
  325.8 35.2 %shard_map.48 = (bf16[1280,128]{1,0:T(8,128)(2,1)}, bf16[1280,128]{1,0:T(8,128)(2,1)}, bf16[1280,128]{1,0:T(8,128)(2,1)}, bf16[1280,128]{1,0:T(8,128)(2,1)}, bf1...) custom-call(s32[1]{0:T(128)} %bitcast.4.me_ref, ...), custom_call_target="tpu_custom_call" | custom-call | flops 15099494400 | bytes 56115200 | tf_op jit(solution)/shard_map/pallas_call | solution.py:112
  378.3 15.2 %collective-permute-done.35.refs_15_ = bf16[1024,128]{1,0:T(8,128)(2,1)} collective-permute-done((bf16[1024,128]{1,0:T(8,128)(2,1)}, bf16[1024,128]{1,0:T(8,128)(2,1)}, u32[]{:S(2)}, u32[]{:S(2)}) %collective-permute-start.35) | collective-permute-done | bytes 262176 | tf_op jit(solution)/shard_map/ppermute | solution.py:29
  395.5 13.8 %collective-permute-done.37.refs_17_ = bf16[1024,128]{1,0:T(8,128)(2,1)} collective-permute-done((bf16[1024,128]{1,0:T(8,128)(2,1)}, bf16[1024,128]{1,0:T(8,128)(2,1)}, u32[]{:S(2)}, u32[]{:S(2)}) %collective-permute-start.37) | collective-permute-done | bytes 262176 | tf_op jit(solution)/shard_map/ppermute | solution.py:29
  473.3 35.1 %shard_map.50 = (bf16[1280,128]{1,0:T(8,128)(2,1)}, bf16[1280,128]{1,0:T(8,128)(2,1)}, bf16[1280,128]{1,0:T(8,128)(2,1)}, bf16[1280,128]{1,0:T(8,128)(2,1)}, bf1...) custom-call(s32[1]{0:T(128)} %bitcast.4.me_ref, ...), custom_call_target="tpu_custom_call" | custom-call | flops 15099494400 | bytes 56115200 | tf_op jit(solution)/shard_map/pallas_call | solution.py:112
  515.5 18.5 %collective-permute-done.52.refs_17_ = bf16[1280,128]{1,0:T(8,128)(2,1)S(1)} collective-permute-done((bf16[1280,128]{1,0:T(8,128)(2,1)}, bf16[1280,128]{1,0:T(8,128)(2,1)S(1)}, u32[]{:S(2)}, u32[]{:S(2)}) %collective-permute-start.52) | collective-permute-done | bytes 327712 | tf_op jit(solution)/shard_map/ppermute | solution.py:29
  534.0 12.4 %collective-permute-done.53.refs_3_ = bf16[1280,128]{1,0:T(8,128)(2,1)S(1)} collective-permute-done((bf16[1280,128]{1,0:T(8,128)(2,1)}, bf16[1280,128]{1,0:T(8,128)(2,1)S(1)}, u32[]{:S(2)}, u32[]{:S(2)}) %collective-permute-start.53) | collective-permute-done | bytes 327712 | tf_op jit(solution)/shard_map/ppermute | solution.py:29
  550.2 11.7 %collective-permute-done.55.refs_5_ = bf16[1280,128]{1,0:T(8,128)(2,1)S(1)} collective-permute-done((bf16[1280,128]{1,0:T(8,128)(2,1)}, bf16[1280,128]{1,0:T(8,128)(2,1)S(1)}, u32[]{:S(2)}, u32[]{:S(2)}) %collective-permute-start.55) | collective-permute-done | bytes 327712 | tf_op jit(solution)/shard_map/ppermute | solution.py:29
  578.5 11.8 %collective-permute-done.59.refs_9_ = bf16[1280,128]{1,0:T(8,128)(2,1)} collective-permute-done((bf16[1280,128]{1,0:T(8,128)(2,1)}, bf16[1280,128]{1,0:T(8,128)(2,1)}, u32[]{:S(2)}, u32[]{:S(2)}) %collective-permute-start.59) | collective-permute-done | bytes 327712 | tf_op jit(solution)/shard_map/ppermute | solution.py:29
  591.7 29.1 %shard_map.52 = (bf16[768,128]{1,0:T(8,128)(2,1)}, bf16[768,128]{1,0:T(8,128)(2,1)}, bf16[768,128]{1,0:T(8,128)(2,1)}, bf16[768,128]{1,0:T(8,128)(2,1)}, bf16[76...) custom-call(s32[1]{0:T(128)} %bitcast.4.me_ref, ...), custom_call_target="tpu_custom_call" | custom-call | flops 9059696640 | bytes 52543488 | tf_op jit(solution)/shard_map/pallas_call | solution.py:112
  626.2 26.3 %shard_map.53 = (bf16[512,128]{1,0:T(8,128)(2,1)}, bf16[512,128]{1,0:T(8,128)(2,1)}, bf16[512,128]{1,0:T(8,128)(2,1)}, bf16[512,128]{1,0:T(8,128)(2,1)}, bf16[51...) custom-call(s32[1]{0:T(128)} %bitcast.4.me_ref, ...), custom_call_target="tpu_custom_call" | custom-call | flops 6039797760 | bytes 50757632 | tf_op jit(solution)/shard_map/pallas_call | solution.py:112
  708.8 11.2 %collective-permute-done.72.refs_7_ = bf16[768,128]{1,0:T(8,128)(2,1)S(1)} collective-permute-done((bf16[768,128]{1,0:T(8,128)(2,1)S(1)}, bf16[768,128]{1,0:T(8,128)(2,1)S(1)}, u32[]{:S(2)}, u32[]{:S(2)}) %collective-permute-start.72) | collective-permute-done | bytes 196640 | tf_op jit(solution)/shard_map/ppermute | solution.py:29
  723.6 13.9 %shard_map.56.refs_18_ = f32[2048,5760]{1,0:T(8,128)} custom-call(bf16[16,2048,128]{2,1,0:T(8,128)(2,1)} %constant_dynamic-update-slice_fusion.refs_0_, f32[2048,256]{1,0:T(8,128)} %pad.4.refs_1_, bf16[1024,128]{1,0:T(8,128)(2,1)} %get-tuple-element.533.refs_2_, bf16[1024,128]{1,0:T(8,128)(2,1)} %collective-permute-done.23.refs_3_, ...), custom_call_target="tpu_custom_call", output_to_operand_aliasing={{}: (18, {})} | custom-call | flops 8589934592 | bytes 20971520 | tf_op jit(solution)/shard_map/pallas_call | solution.py:157
  743.4 16.6 %shard_map.57.refs_18_ = f32[2048,5760]{1,0:T(8,128)} custom-call(bf16[16,2048,128]{2,1,0:T(8,128)(2,1)} %constant_dynamic-update-slice_fusion.refs_0_, f32[2048,256]{1,0:T(8,128)} %pad.4.refs_1_, bf16[1280,128]{1,0:T(8,128)(2,1)} %get-tuple-element.517.refs_2_, bf16[1280,128]{1,0:T(8,128)(2,1)} %copy-done.2, ...), custom_call_target="tpu_custom_call", output_to_operand_aliasing={{}: (18, {})} | custom-call | flops 10737418240 | bytes 24117248 | tf_op jit(solution)/shard_map/pallas_call | solution.py:157
  767.4 25.3 %shard_map.54 = (bf16[384,128]{1,0:T(8,128)(2,1)}, bf16[384,128]{1,0:T(8,128)(2,1)}, bf16[384,128]{1,0:T(8,128)(2,1)}, bf16[384,128]{1,0:T(8,128)(2,1)}, bf16[38...) custom-call(s32[1]{0:T(128)} %bitcast.4.me_ref, ...), custom_call_target="tpu_custom_call" | custom-call | flops 4529848320 | bytes 49864704 | tf_op jit(solution)/shard_map/pallas_call | solution.py:112
  803.4 16.6 %shard_map.58.refs_18_ = f32[2048,5760]{1,0:T(8,128)} custom-call(bf16[16,2048,128]{2,1,0:T(8,128)(2,1)} %constant_dynamic-update-slice_fusion.refs_0_, f32[2048,256]{1,0:T(8,128)} %pad.4.refs_1_, bf16[1280,128]{1,0:T(8,128)(2,1)} %get-tuple-element.501.refs_2_, bf16[1280,128]{1,0:T(8,128)(2,1)} %copy-done.8, ...), custom_call_target="tpu_custom_call", output_to_operand_aliasing={{}: (18, {})} | custom-call | flops 10737418240 | bytes 24117248 | tf_op jit(solution)/shard_map/pallas_call | solution.py:157
  826.8 11.9 %shard_map.59.refs_18_ = f32[2048,5760]{1,0:T(8,128)} custom-call(bf16[16,2048,128]{2,1,0:T(8,128)(2,1)} %constant_dynamic-update-slice_fusion.refs_0_, f32[2048,256]{1,0:T(8,128)} %pad.4.refs_1_, bf16[768,128]{1,0:T(8,128)(2,1)} %get-tuple-element.485.refs_2_, bf16[768,128]{1,0:T(8,128)(2,1)} %copy-done.32, ...), custom_call_target="tpu_custom_call", output_to_operand_aliasing={{}: (18, {})} | custom-call | flops 6442450944 | bytes 17825792 | tf_op jit(solution)/shard_map/pallas_call | solution.py:157
  (483 shorter events, 343.4 us)
Async XLA Ops:
  6.5 221.9 %all-gather.5.cloned.1.call-start = ((), (), s32[]{:S(2)}) async-start(), calls=%async_computation.1 | async-start | bytes 3203072 | tf_op jit(solution)/shard_map/all_gather | solution.py:191
  10.1 315.7 %all-gather.3.cloned.1.call-start = ((), (), s32[]{:S(2)}) async-start(), calls=%async_computation | async-start | bytes 13613056 | tf_op jit(solution)/shard_map/all_gather | solution.py:191
  76.7 52.5 %collective-permute-start.5 = (bf16[2,2048,128]{2,1,0:T(8,128)(2,1)S(1)}, bf16[2,2048,128]{2,1,0:T(8,128)(2,1)S(1)}, u32[]{:S(2)}, u32[]{:S(2)}) collective-permute-start(bf16[2,2048,128]{2,1,0:T(8,128)(2,1)S(1)} %pad_maximum_fusion.3), channel_id=1, source_target_pairs={{0,8},{2,10},{4,12},{6,14},{8,0},{10,2},{12,4},{14,6},{16,24},{18,... | collective-permute-start | bytes 3145736 | tf_op jit(solution)/shard_map/ppermute | solution.py:29
  130.7 157.5 %collective-permute-start.6 = (bf16[4,2048,128]{2,1,0:T(8,128)(2,1)}, bf16[4,2048,128]{2,1,0:T(8,128)(2,1)}, u32[]{:S(2)}, u32[]{:S(2)}) collective-permute-start(bf16[4,2048,128]{2,1,0:T(8,128)(2,1)} %pad_maximum_fusion.1), channel_id=1, source_target_pairs={{0,4},{2,6},{4,0},{6,2},{8,12},{10,14},{12,8},{14,10},{16,20},{18,... | collective-permute-start | bytes 6291464 | tf_op jit(solution)/shard_map/ppermute | solution.py:29
  161.3 61.0 %collective-permute-start.11 = (bf16[512,128]{1,0:T(8,128)(2,1)}, bf16[512,128]{1,0:T(8,128)(2,1)}, u32[]{:S(2)}, u32[]{:S(2)}) collective-permute-start(bf16[512,128]{1,0:T(8,128)(2,1)} %get-tuple-element.308), channel_id=1, source_target_pairs={{0,4},{2,6},{4,0},{6,2},{8,12},{10,14},{12,8},{14,10},{16,20},{18,... | collective-permute-start | bytes 393224 | tf_op jit(solution)/shard_map/ppermute | solution.py:29
  167.1 57.5 %collective-permute-start.12 = (bf16[512,128]{1,0:T(8,128)(2,1)}, bf16[512,128]{1,0:T(8,128)(2,1)}, u32[]{:S(2)}, u32[]{:S(2)}) collective-permute-start(bf16[512,128]{1,0:T(8,128)(2,1)} %get-tuple-element.309), channel_id=1, source_target_pairs={{0,20},{2,22},{4,16},{6,18},{8,28},{10,30},{12,24},{14,26},{16,4},... | collective-permute-start | bytes 393224 | tf_op jit(solution)/shard_map/ppermute | solution.py:29
  169.1 56.1 %collective-permute-start.13 = (bf16[512,128]{1,0:T(8,128)(2,1)}, bf16[512,128]{1,0:T(8,128)(2,1)}, u32[]{:S(2)}, u32[]{:S(2)}) collective-permute-start(bf16[512,128]{1,0:T(8,128)(2,1)} %get-tuple-element.310), channel_id=1, source_target_pairs={{0,12},{2,14},{4,8},{6,10},{8,4},{10,6},{12,0},{14,2},{16,28},{18,... | collective-permute-start | bytes 393224 | tf_op jit(solution)/shard_map/ppermute | solution.py:29
  181.0 45.8 %collective-permute-start.14 = (bf16[512,128]{1,0:T(8,128)(2,1)}, bf16[512,128]{1,0:T(8,128)(2,1)}, u32[]{:S(2)}, u32[]{:S(2)}) collective-permute-start(bf16[512,128]{1,0:T(8,128)(2,1)} %get-tuple-element.311), channel_id=1, source_target_pairs={{0,28},{2,30},{4,24},{6,26},{8,20},{10,22},{12,16},{14,18},{16,12}... | collective-permute-start | bytes 393224 | tf_op jit(solution)/shard_map/ppermute | solution.py:29
  293.1 67.8 %collective-permute-start.29 = (bf16[1024,128]{1,0:T(8,128)(2,1)}, bf16[1024,128]{1,0:T(8,128)(2,1)}, u32[]{:S(2)}, u32[]{:S(2)}) collective-permute-start(bf16[1024,128]{1,0:T(8,128)(2,1)} %get-tuple-element.345), channel_id=1, source_target_pairs={{0,28},{2,30},{4,24},{6,26},{8,20},{10,22},{12,16},{14,18},{16,12}... | collective-permute-start | bytes 786440 | tf_op jit(solution)/shard_map/ppermute | solution.py:29
  305.1 58.0 %collective-permute-start.30 = (bf16[1024,128]{1,0:T(8,128)(2,1)}, bf16[1024,128]{1,0:T(8,128)(2,1)S(1)}, u32[]{:S(2)}, u32[]{:S(2)}) collective-permute-start(bf16[1024,128]{1,0:T(8,128)(2,1)} %get-tuple-element.346), channel_id=1, source_target_pairs={{0,2},{2,0},{4,6},{6,4},{8,10},{10,8},{12,14},{14,12},{16,18},{18,... | collective-permute-start | bytes 786440 | tf_op jit(solution)/shard_map/ppermute | solution.py:29
  308.0 55.1 %collective-permute-start.31 = (bf16[1024,128]{1,0:T(8,128)(2,1)}, bf16[1024,128]{1,0:T(8,128)(2,1)S(1)}, u32[]{:S(2)}, u32[]{:S(2)}) collective-permute-start(bf16[1024,128]{1,0:T(8,128)(2,1)} %get-tuple-element.347), channel_id=1, source_target_pairs={{0,18},{2,16},{4,22},{6,20},{8,26},{10,24},{12,30},{14,28},{16,2},... | collective-permute-start | bytes 786440 | tf_op jit(solution)/shard_map/ppermute | solution.py:29
  321.8 43.0 %collective-permute-start.32 = (bf16[1024,128]{1,0:T(8,128)(2,1)}, bf16[1024,128]{1,0:T(8,128)(2,1)S(1)}, u32[]{:S(2)}, u32[]{:S(2)}) collective-permute-start(bf16[1024,128]{1,0:T(8,128)(2,1)} %get-tuple-element.348), channel_id=1, source_target_pairs={{0,10},{2,8},{4,14},{6,12},{8,2},{10,0},{12,6},{14,4},{16,26},{18,... | collective-permute-start | bytes 786440 | tf_op jit(solution)/shard_map/ppermute | solution.py:29
  361.0 48.3 %collective-permute-start.38 = (bf16[1280,128]{1,0:T(8,128)(2,1)}, bf16[1280,128]{1,0:T(8,128)(2,1)S(1)}, u32[]{:S(2)}, u32[]{:S(2)}) collective-permute-start(bf16[1280,128]{1,0:T(8,128)(2,1)} %get-tuple-element.372), channel_id=1, source_target_pairs={{0,16},{2,18},{4,20},{6,22},{8,24},{10,26},{12,28},{14,30},{16,0},... | collective-permute-start | bytes 983048 | tf_op jit(solution)/shard_map/ppermute | solution.py:29
  366.8 42.5 %collective-permute-start.37 = (bf16[1024,128]{1,0:T(8,128)(2,1)}, bf16[1024,128]{1,0:T(8,128)(2,1)}, u32[]{:S(2)}, u32[]{:S(2)}) collective-permute-start(bf16[1024,128]{1,0:T(8,128)(2,1)} %get-tuple-element.353), channel_id=1, source_target_pairs={{0,30},{2,28},{4,26},{6,24},{8,22},{10,20},{12,18},{14,16},{16,14}... | collective-permute-start | bytes 786440 | tf_op jit(solution)/shard_map/ppermute | solution.py:29
  371.6 42.7 %collective-permute-start.39 = (bf16[1280,128]{1,0:T(8,128)(2,1)}, bf16[1280,128]{1,0:T(8,128)(2,1)S(1)}, u32[]{:S(2)}, u32[]{:S(2)}) collective-permute-start(bf16[1280,128]{1,0:T(8,128)(2,1)} %get-tuple-element.373), channel_id=1, source_target_pairs={{0,8},{2,10},{4,12},{6,14},{8,0},{10,2},{12,4},{14,6},{16,24},{18,... | collective-permute-start | bytes 983048 | tf_op jit(solution)/shard_map/ppermute | solution.py:29
  414.3 242.0 %collective-permute-start.7 = (bf16[8,2048,128]{2,1,0:T(8,128)(2,1)}, bf16[8,2048,128]{2,1,0:T(8,128)(2,1)}, u32[]{:S(2)}, u32[]{:S(2)}) collective-permute-start(bf16[8,2048,128]{2,1,0:T(8,128)(2,1)} %pad_maximum_fusion), channel_id=1, source_target_pairs={{0,2},{2,0},{4,6},{6,4},{8,10},{10,8},{12,14},{14,12},{16,18},{18,... | collective-permute-start | bytes 12582920 | tf_op jit(solution)/shard_map/ppermute | solution.py:29
  450.7 57.8 %collective-permute-start.48 = (bf16[1280,128]{1,0:T(8,128)(2,1)}, bf16[1280,128]{1,0:T(8,128)(2,1)S(1)}, u32[]{:S(2)}, u32[]{:S(2)}) collective-permute-start(bf16[1280,128]{1,0:T(8,128)(2,1)} %get-tuple-element.382), channel_id=1, source_target_pairs={{0,26},{2,24},{4,30},{6,28},{8,18},{10,16},{12,22},{14,20},{16,10}... | collective-permute-start | bytes 983048 | tf_op jit(solution)/shard_map/ppermute | solution.py:29
  450.7 59.8 %collective-permute-start.49 = (bf16[1280,128]{1,0:T(8,128)(2,1)}, bf16[1280,128]{1,0:T(8,128)(2,1)S(1)}, u32[]{:S(2)}, u32[]{:S(2)}) collective-permute-start(bf16[1280,128]{1,0:T(8,128)(2,1)} %get-tuple-element.383), channel_id=1, source_target_pairs={{0,6},{2,4},{4,2},{6,0},{8,14},{10,12},{12,10},{14,8},{16,22},{18,... | collective-permute-start | bytes 983048 | tf_op jit(solution)/shard_map/ppermute | solution.py:29
  455.3 57.0 %collective-permute-start.50 = (bf16[1280,128]{1,0:T(8,128)(2,1)}, bf16[1280,128]{1,0:T(8,128)(2,1)S(1)}, u32[]{:S(2)}, u32[]{:S(2)}) collective-permute-start(bf16[1280,128]{1,0:T(8,128)(2,1)} %get-tuple-element.384), channel_id=1, source_target_pairs={{0,22},{2,20},{4,18},{6,16},{8,30},{10,28},{12,26},{14,24},{16,6},... | collective-permute-start | bytes 983048 | tf_op jit(solution)/shard_map/ppermute | solution.py:29
  465.9 47.6 %collective-permute-start.51 = (bf16[1280,128]{1,0:T(8,128)(2,1)}, bf16[1280,128]{1,0:T(8,128)(2,1)S(1)}, u32[]{:S(2)}, u32[]{:S(2)}) collective-permute-start(bf16[1280,128]{1,0:T(8,128)(2,1)} %get-tuple-element.385), channel_id=1, source_target_pairs={{0,14},{2,12},{4,10},{6,8},{8,6},{10,4},{12,2},{14,0},{16,30},{18,... | collective-permute-start | bytes 983048 | tf_op jit(solution)/shard_map/ppermute | solution.py:29
  513.5 48.4 %collective-permute-start.55 = (bf16[1280,128]{1,0:T(8,128)(2,1)}, bf16[1280,128]{1,0:T(8,128)(2,1)S(1)}, u32[]{:S(2)}, u32[]{:S(2)}) collective-permute-start(bf16[1280,128]{1,0:T(8,128)(2,1)} %get-tuple-element.407), channel_id=1, source_target_pairs={{0,24},{2,26},{4,28},{6,30},{8,16},{10,18},{12,20},{14,22},{16,8},... | collective-permute-start | bytes 983048 | tf_op jit(solution)/shard_map/ppermute | solution.py:29
  565.3 55.5 %collective-permute-start.60 = (bf16[1280,128]{1,0:T(8,128)(2,1)}, bf16[1280,128]{1,0:T(8,128)(2,1)S(1)}, u32[]{:S(2)}, u32[]{:S(2)}) collective-permute-start(bf16[1280,128]{1,0:T(8,128)(2,1)} %get-tuple-element.412), channel_id=1, source_target_pairs={{0,2},{2,0},{4,6},{6,4},{8,10},{10,8},{12,14},{14,12},{16,18},{18,... | collective-permute-start | bytes 983048 | tf_op jit(solution)/shard_map/ppermute | solution.py:29
  574.4 46.6 %collective-permute-start.61 = (bf16[1280,128]{1,0:T(8,128)(2,1)}, bf16[1280,128]{1,0:T(8,128)(2,1)S(1)}, u32[]{:S(2)}, u32[]{:S(2)}) collective-permute-start(bf16[1280,128]{1,0:T(8,128)(2,1)} %get-tuple-element.413), channel_id=1, source_target_pairs={{0,18},{2,16},{4,22},{6,20},{8,26},{10,24},{12,30},{14,28},{16,2},... | collective-permute-start | bytes 983048 | tf_op jit(solution)/shard_map/ppermute | solution.py:29
  578.5 42.6 %collective-permute-start.62 = (bf16[1280,128]{1,0:T(8,128)(2,1)}, bf16[1280,128]{1,0:T(8,128)(2,1)S(1)}, u32[]{:S(2)}, u32[]{:S(2)}) collective-permute-start(bf16[1280,128]{1,0:T(8,128)(2,1)} %get-tuple-element.414), channel_id=1, source_target_pairs={{0,10},{2,8},{4,14},{6,12},{8,2},{10,0},{12,6},{14,4},{16,26},{18,... | collective-permute-start | bytes 983048 | tf_op jit(solution)/shard_map/ppermute | solution.py:29
  (210 other events, 5501.5 us)
Sparse Core Ops, SparseCore 0:
  10.2 53.8 all-gather.4
  66.3 174.1 all-gather.2

commit v3 on v2

--- a/solution.py
+++ b/solution.py
@@ -9,8 +9,9 @@
 
 
 LANES = 128
-WEIGHTS = (4, 8, 10, 10, 6, 4, 3)
-GROUPS = (0, 1, 2)
+SUBLANES = 16
+WEIGHTS = (6, 8, 6, 10, 8, 4, 3)
+GROUPS = (0, 1, 3)
 VMEM = 60 * 1024 * 1024
 
 
@@ -22,6 +23,10 @@
 
 def full_tiles(columns):
     return -(-columns // LANES) * LANES
+
+
+def full_rows(rows):
+    return -(-rows // SUBLANES) * SUBLANES
 
 
 def exchange(block, flip):
@@ -40,13 +45,22 @@
     return order
 
 
-def gather_absolute(block):
-    me = lax.axis_index("rows")
-    for bit in far_bits(lax.axis_size("rows")):
+def spread(block, gate=None):
+    *bits, last = far_bits(lax.axis_size("rows"))
+    for n, bit in enumerate(bits):
         other = exchange(block, bit)
-        low = (me & bit) == 0
-        block = jnp.concatenate([jnp.where(low, block, other), jnp.where(low, other, block)])
-    return block
+        if gate is not None and n == 0:
+            other, _ = lax.optimization_barrier((other, gate))
+        block = jnp.concatenate([block, other])
+    return block, exchange(block, last)
+
+
+def turn_kernel(basis_ref, out_ref):
+    out_ref[...] = basis_ref[...].T
+
+
+def turn(basis):
+    return pl.pallas_call(turn_kernel, out_shape=jax.ShapeDtypeStruct(basis.shape[::-1], basis.dtype))(basis)
 
 
 def arrange_kernel(devices, spans, basis_ref, *outs):
@@ -56,10 +70,13 @@
         pieces = []
         for begin, count in group:
             pieces += [whole[:, owner * span + begin : owner * span + begin + count] for owner in range(devices)]
-        blank = out_ref.shape[2] - sum(piece.shape[1] for piece in pieces)
+        blank = out_ref.shape[1] - sum(piece.shape[1] for piece in pieces)
         if blank:
             pieces.append(jnp.zeros((whole.shape[0], blank), jnp.float32))
-        out_ref[0] = jnp.concatenate(pieces, axis=1).astype(jnp.bfloat16)
+        rows = whole.shape[0]
+        out_ref[:rows, :] = jnp.concatenate(pieces, axis=1).astype(jnp.bfloat16)
+        if rows < out_ref.shape[0]:
+            out_ref[rows:, :] = jnp.zeros((out_ref.shape[0] - rows, out_ref.shape[1]), jnp.bfloat16)
 
 
 def arrange(in_basis, devices, spans):
@@ -67,24 +84,29 @@
     return pl.pallas_call(
         functools.partial(arrange_kernel, devices, spans),
         out_shape=[
-            jax.ShapeDtypeStruct((1, rows, full_tiles(devices * sum(count for _, count in group))), jnp.bfloat16)
+            jax.ShapeDtypeStruct((full_rows(rows), full_tiles(devices * sum(count for _, count in group))), jnp.bfloat16)
             for group in spans
         ],
         compiler_params=pltpu.CompilerParams(vmem_limit_bytes=VMEM),
     )(in_basis)
 
 
-def rotate_kernel(columns, grads, sources, order, me_ref, *refs):
-    basis_ref, grad_ref = refs[:2]
-    outs = refs[2 : 2 + len(order)]
+def rotate_kernel(columns, part, grads, order, me_ref, *refs):
+    own_ref, other_ref, grad_ref = refs[:3]
+    outs = refs[3 : 3 + len(order)]
     stage, basis_t, rows, pair = refs[-4:]
     step = pl.program_id(0)
-    part = basis_ref.shape[1]
+    pitch = full_rows(part)
 
     @pl.when(step == 0)
     def _():
-        for slot, source in enumerate(sources):
-            stage[source * part : (source + 1) * part, :] = basis_ref[slot].astype(jnp.float32)
+        even = me_ref[0] % 2 == 0
+        for slot, offset in enumerate(order[: len(order) // 2]):
+            block = slice(slot * pitch, slot * pitch + part)
+            own, other = own_ref[block, :].astype(jnp.float32), other_ref[block, :].astype(jnp.float32)
+            both = jnp.concatenate([jnp.where(even, own, other), jnp.where(even, other, own)])
+            start = pl.multiple_of((me_ref[0] ^ offset) // 2 * (2 * part), 8)
+            stage[pl.ds(start, 2 * part), :] = both
         basis_t[...] = stage[...].T.astype(jnp.bfloat16)
 
     pair[:, :LANES] = grad_ref[0].astype(jnp.bfloat16)
@@ -101,20 +123,21 @@
             out_ref[...] = rows[pl.ds(pl.multiple_of(owner * height, LANES), height), :].astype(jnp.bfloat16)
 
 
-def rotate(me, basis, begin, columns, grad, grads, sources, order):
-    devices, part, _ = basis.shape
-    depth = devices * part
+def rotate(me, basis, begin, columns, grad, grads, order):
+    devices = len(order)
+    depth = grad.shape[1]
+    part = depth // devices
     height = columns // devices * grads
     wide = full_tiles(columns)
     basis_spec = pl.BlockSpec(
-        (pl.Element(devices), pl.Element(part), pl.Element(wide)), lambda step, me: (0, 0, begin)
-    )
-    return pl.pallas_call(
-        functools.partial(rotate_kernel, columns, grads, sources, order),
+        (pl.Element(basis[0].shape[0]), pl.Element(wide)), lambda step, me: (0, begin)
+    )
+    return pl.pallas_call(
+        functools.partial(rotate_kernel, columns, part, grads, order),
         grid_spec=pltpu.PrefetchScalarGridSpec(
             num_scalar_prefetch=1,
             grid=(grads // 2,),
-            in_specs=[basis_spec, pl.BlockSpec((2, depth, LANES), lambda step, me: (step, 0, 0))],
+            in_specs=[basis_spec, basis_spec, pl.BlockSpec((2, depth, LANES), lambda step, me: (step, 0, 0))],
             out_specs=[pl.BlockSpec((height, LANES), lambda step, me: (0, 0))] * devices,
             scratch_shapes=[
                 pltpu.VMEM((depth, wide), jnp.float32),
@@ -130,13 +153,28 @@
             bytes_accessed=4 * grads * depth * LANES + 2 * columns * (depth + grads * LANES),
             transcendentals=0,
         ),
-    )(me, basis, grad)
+    )(me, *basis, grad)
+
+
+def eigen_kernel(seeds_ref, out_ref):
+    rows = seeds_ref.shape[0]
+    eigval = jnp.exp2(seeds_ref[...].astype(jnp.float32) * 0.125 - 4.0)
+    out_ref[:rows, :] = 1.0 / (eigval + 0.1)
+    if rows < out_ref.shape[0]:
+        out_ref[rows:, :] = jnp.zeros((out_ref.shape[0] - rows, out_ref.shape[1]), jnp.float32)
+
+
+def eigen(eigen_seeds):
+    return pl.pallas_call(
+        eigen_kernel,
+        out_shape=jax.ShapeDtypeStruct((full_tiles(eigen_seeds.shape[0]), eigen_seeds.shape[1]), jnp.float32),
+    )(eigen_seeds)
 
 
 def finish_kernel(begin, grads, devices, *refs):
-    basis_ref, scale_ref, out_ref = refs[0], refs[1], refs[-1]
-    moved = jnp.concatenate([ref[...] for ref in refs[2 : 2 + devices]], axis=1)
-    basis = jnp.concatenate([basis_ref[slot] for slot in range(devices)], axis=1)
+    own_ref, other_ref, scale_ref, out_ref = refs[0], refs[1], refs[2], refs[-1]
+    moved = jnp.concatenate([ref[...] for ref in refs[3 : 3 + devices]], axis=1)
+    basis = jnp.concatenate([ref[slot] for ref in (own_ref, other_ref) for slot in range(devices // 2)], axis=1)
     both = lax.dot_general(basis, moved, (((1,), (1,)), ((), ())), preferred_element_type=jnp.float32)
     per_block = LANES // grads
     height = both.shape[0]
@@ -150,7 +188,8 @@
 
 
 def finish(basis, scale, moved, result, begin, span, grads):
-    devices, width_out, _ = basis.shape
+    half, width_out, _ = basis[0].shape
+    devices = 2 * half
     height, _ = moved[0].shape
     tile = width_out // 4
     aliased = [] if result is None else [result]
@@ -158,21 +197,22 @@
         functools.partial(finish_kernel, begin, grads, devices),
         grid=(width_out // tile,),
         in_specs=[
-            pl.BlockSpec((devices, tile, LANES), lambda row: (0, row, 0)),
+            pl.BlockSpec((half, tile, LANES), lambda row: (0, row, 0)),
+            pl.BlockSpec((half, tile, LANES), lambda row: (0, row, 0)),
             pl.BlockSpec((tile, scale.shape[1]), lambda row: (row, 0)),
         ]
         + [pl.BlockSpec((height, LANES), lambda row: (0, 0))] * devices
         + [pl.BlockSpec(memory_space=pl.ANY)] * len(aliased),
         out_specs=pl.BlockSpec((pl.Element(tile), pl.Element(height)), lambda row: (row * tile, begin * grads)),
         out_shape=jax.ShapeDtypeStruct((width_out, span * grads), jnp.float32),
-        input_output_aliases={2 + devices: 0} if aliased else {},
+        input_output_aliases={3 + devices: 0} if aliased else {},
         compiler_params=pltpu.CompilerParams(vmem_limit_bytes=VMEM),
         cost_estimate=pl.CostEstimate(
             flops=2 * width_out * height * devices * LANES,
-            bytes_accessed=2 * basis.size + 2 * devices * height * LANES + 4 * width_out * height,
+            bytes_accessed=4 * basis[0].size + 2 * devices * height * LANES + 4 * width_out * height,
             transcendentals=0,
         ),
-    )(basis, scale, *moved, *aliased)
+    )(*basis, scale, *moved, *aliased)
 
 
 def pipelined(gradients, in_basis, out_basis, eigen_seeds):
@@ -188,25 +228,19 @@
     me = lax.axis_index("rows").astype(jnp.int32)[None]
 
     (early,) = arrange(in_basis, devices, spans[:1])
-    gathered = [lax.all_gather(block, "rows", axis=0, tiled=True) for block in arrange(in_basis, devices, spans[1:])]
-    early = gather_absolute(early)
-    early, out_basis = lax.optimization_barrier((early, out_basis))
-    gathered = [early] + gathered
-    basis = out_basis.T[None]
-    denom = jnp.exp2(eigen_seeds.astype(jnp.float32) * 0.125 - 4.0) + 0.1
-    scale = jnp.pad((1.0 / denom).T, ((0, 0), (0, -span % LANES)))
-    for n, bit in enumerate(far_bits(devices)):
-        incoming = exchange(basis, bit)
-        basis = jnp.concatenate([basis, incoming])
-
+    middle, late = arrange(in_basis, devices, spans[1:])
+    early = spread(early)
+    gathered = [early, spread(middle, early[0]), spread(late)]
+    basis = [block.reshape(devices // 2, -1, LANES) for block in spread(turn(out_basis))]
+    scale = eigen(eigen_seeds)
+    scale = turn(scale)
     grad = gradients.transpose(1, 2, 0)
     far = sorted(range(devices), key=lambda slot: -order[slot])
     moved = []
     for n, (begin, count) in enumerate(chunks):
         group = max(index for index, low in enumerate(GROUPS) if low <= n)
         column = (begin - begins[GROUPS[group]]) * devices
-        sources = list(range(devices)) if group else order
-        rotated = rotate(me, gathered[group], column, count * devices, grad, grads, sources, order)
+        rotated = rotate(me, gathered[group], column, count * devices, grad, grads, order)
         if n > 1:
             rotated, moved[n - 2], grad = lax.optimization_barrier((rotated, moved[n - 2], grad))
         arrived = {slot: exchange(rotated[slot], order[slot]) if order[slot] else rotated[slot] for slot in far}

time: 885 us -> 918 us (1.037)
  waiting for transfers between devices: 328 us -> 381 us
  starting transfers between devices: 202 us -> 168 us
  other arithmetic: 8.42 us -> 22.8 us
  between operations: 15.1 us -> 2.28 us
  Pallas kernels: 304 us -> 316 us
    ppermute x113 -> x121, waiting for transfers between devices: 327 us -> 381 us  [exchange(): lax.ppermute(block, 'rows', [(source, source ^ flip) for source in range(...]
    ppermute x113 -> x121, starting transfers between devices: 202 us -> 168 us  [exchange(): lax.ppermute(block, 'rows', [(source, source ^ flip) for source in range(...]
    concatenate x7 -> x10, other arithmetic: 6.64 us -> 22.8 us  [spread(): block = jnp.concatenate([block, other])]
    pallas_call x7 -> x10, Pallas kernels: 211 us -> 223 us  [the longest x7 215 us: rotate(): pl.pallas_call(functools.partial(rotate_kernel, columns, part, grads, ord...]
  transfers between devices with their start and end apart: 115 -> 121, of which waited for: 32 -> 32; matrix products, arithmetic and copies ran while one was open for 3% -> 4% of each run, Pallas kernels for 33% -> 34%
where the time goes in v3:
time: 918 us; the launch traced here: 906 us
  waiting for transfers between devices  381 us (42%)
  Pallas kernels  316 us (34%)
  starting transfers between devices  168 us (18%)
  other arithmetic  22.8 us (2%)
  local copies, waits for them, and re-layouts  16.2 us (2%)
    ppermute x121, waiting for transfers between devices, exchange(): lax.ppermute(block, 'rows', [(source, source ^ flip) for source in range(...  381 us
    pallas_call x7, Pallas kernels, rotate(): pl.pallas_call(functools.partial(rotate_kernel, columns, part, grads, ord...  215 us
    ppermute x121, starting transfers between devices, exchange(): lax.ppermute(block, 'rows', [(source, source ^ flip) for source in range(...  168 us
    pallas_call x7, Pallas kernels, finish(): pl.pallas_call(functools.partial(finish_kernel, begin, grads, devices), g...  86.8 us
    concatenate x10, other arithmetic, spread(): block = jnp.concatenate([block, other])  22.8 us
  transfers between devices with their start and end apart: 121, of which 32 were waited for; matrix products, arithmetic and copies ran while one was open for 4% of the time, Pallas kernels for 34%

profile of v3, /device:TPU:11, one launch (start us, length us, event | category | flops | bytes accessed | tf_op | source)
XLA Modules:
  0.0 906.3 jit_solution(7299434973807249586)
XLA Ops:
  36.3 21.2 %collective-permute-done.8 = bf16[192,896]{1,0:T(8,128)(2,1)S(1)} collective-permute-done((bf16[192,896]{1,0:T(8,128)(2,1)}, bf16[192,896]{1,0:T(8,128)(2,1)S(1)}, u32[]{:S(2)}, u32[]{:S(2)}) %collective-permute-start.8) | collective-permute-done | bytes 344096 | tf_op jit(solution)/shard_map/ppermute | solution.py:34
  58.7 12.5 %collective-permute-done.4 = bf16[192,1664]{1,0:T(8,128)(2,1)S(1)} collective-permute-done((bf16[192,1664]{1,0:T(8,128)(2,1)}, bf16[192,1664]{1,0:T(8,128)(2,1)S(1)}, u32[]{:S(2)}, u32[]{:S(2)}) %collective-permute-start.4) | collective-permute-done | bytes 639008 | tf_op jit(solution)/shard_map/ppermute | solution.py:34
  78.3 17.6 %collective-permute-done.12 = bf16[384,896]{1,0:T(8,128)(2,1)S(1)} collective-permute-done((bf16[384,896]{1,0:T(8,128)(2,1)S(1)}, bf16[384,896]{1,0:T(8,128)(2,1)S(1)}, u32[]{:S(2)}, u32[]{:S(2)}) %collective-permute-start.12) | collective-permute-done | bytes 688160 | tf_op jit(solution)/shard_map/ppermute | solution.py:34
  101.2 14.5 %collective-permute-done = bf16[2048,128]{1,0:T(8,128)(2,1)} collective-permute-done((bf16[2048,128]{1,0:T(8,128)(2,1)}, bf16[2048,128]{1,0:T(8,128)(2,1)}, u32[]{:S(2)}, u32[]{:S(2)}) %collective-permute-start) | collective-permute-done | bytes 524320 | tf_op jit(solution)/shard_map/ppermute | solution.py:34
  132.0 30.1 %shard_map.52 = (bf16[768,128]{1,0:T(8,128)(2,1)}, bf16[768,128]{1,0:T(8,128)(2,1)}, bf16[768,128]{1,0:T(8,128)(2,1)}, bf16[768,128]{1,0:T(8,128)(2,1)}, bf16[76...) custom-call(s32[1]{0:T(128)} %bitcast.2.me_ref, ...), custom_call_target="tpu_custom_call" | custom-call | flops 9059696640 | bytes 52543488 | tf_op jit(solution)/shard_map/pallas_call | solution.py:135
  184.1 53.0 %collective-permute-done.19.refs_7_ = bf16[768,128]{1,0:T(8,128)(2,1)} collective-permute-done((bf16[768,128]{1,0:T(8,128)(2,1)S(1)}, bf16[768,128]{1,0:T(8,128)(2,1)}, u32[]{:S(2)}, u32[]{:S(2)}) %collective-permute-start.19) | collective-permute-done | bytes 196640 | tf_op jit(solution)/shard_map/ppermute | solution.py:34
  279.2 29.7 %shard_map.51 = (bf16[768,128]{1,0:T(8,128)(2,1)}, bf16[768,128]{1,0:T(8,128)(2,1)}, bf16[768,128]{1,0:T(8,128)(2,1)}, bf16[768,128]{1,0:T(8,128)(2,1)}, bf16[76...) custom-call(s32[1]{0:T(128)} %bitcast.2.me_ref, ...), custom_call_target="tpu_custom_call" | custom-call | flops 9059696640 | bytes 52543488 | tf_op jit(solution)/shard_map/pallas_call | solution.py:135
  323.1 33.1 %shard_map.54 = (bf16[1024,128]{1,0:T(8,128)(2,1)}, bf16[1024,128]{1,0:T(8,128)(2,1)}, bf16[1024,128]{1,0:T(8,128)(2,1)}, bf16[1024,128]{1,0:T(8,128)(2,1)}, bf1...) custom-call(s32[1]{0:T(128)} %bitcast.2.me_ref, ...), custom_call_target="tpu_custom_call" | custom-call | flops 12079595520 | bytes 54329344 | tf_op jit(solution)/shard_map/pallas_call | solution.py:135
  361.0 29.9 %collective-permute-done.52.refs_10_ = bf16[768,128]{1,0:T(8,128)(2,1)S(1)} collective-permute-done((bf16[768,128]{1,0:T(8,128)(2,1)S(1)}, bf16[768,128]{1,0:T(8,128)(2,1)S(1)}, u32[]{:S(2)}, u32[]{:S(2)}) %collective-permute-start.52) | collective-permute-done | bytes 196640 | tf_op jit(solution)/shard_map/ppermute | solution.py:34
  396.3 16.7 %collective-permute-done.34.refs_7_ = bf16[1024,128]{1,0:T(8,128)(2,1)S(1)} collective-permute-done((bf16[1024,128]{1,0:T(8,128)(2,1)}, bf16[1024,128]{1,0:T(8,128)(2,1)S(1)}, u32[]{:S(2)}, u32[]{:S(2)}) %collective-permute-start.34) | collective-permute-done | bytes 262176 | tf_op jit(solution)/shard_map/ppermute | solution.py:34
  430.9 15.3 %collective-permute-done.41.refs_14_ = bf16[1024,128]{1,0:T(8,128)(2,1)S(1)} collective-permute-done((bf16[1024,128]{1,0:T(8,128)(2,1)}, bf16[1024,128]{1,0:T(8,128)(2,1)S(1)}, u32[]{:S(2)}, u32[]{:S(2)}) %collective-permute-start.41) | collective-permute-done | bytes 262176 | tf_op jit(solution)/shard_map/ppermute | solution.py:34
  467.9 36.3 %shard_map.53 = (bf16[1280,128]{1,0:T(8,128)(2,1)}, bf16[1280,128]{1,0:T(8,128)(2,1)}, bf16[1280,128]{1,0:T(8,128)(2,1)}, bf16[1280,128]{1,0:T(8,128)(2,1)}, bf1...) custom-call(s32[1]{0:T(128)} %bitcast.2.me_ref, ...), custom_call_target="tpu_custom_call" | custom-call | flops 15099494400 | bytes 56115200 | tf_op jit(solution)/shard_map/pallas_call | solution.py:135
  510.0 33.1 %shard_map.55 = (bf16[1024,128]{1,0:T(8,128)(2,1)}, bf16[1024,128]{1,0:T(8,128)(2,1)}, bf16[1024,128]{1,0:T(8,128)(2,1)}, bf16[1024,128]{1,0:T(8,128)(2,1)}, bf1...) custom-call(s32[1]{0:T(128)} %bitcast.2.me_ref, ...), custom_call_target="tpu_custom_call" | custom-call | flops 12079595520 | bytes 54329344 | tf_op jit(solution)/shard_map/pallas_call | solution.py:135
  562.4 14.4 %collective-permute-done.78.refs_6_ = bf16[1024,128]{1,0:T(8,128)(2,1)S(1)} collective-permute-done((bf16[1024,128]{1,0:T(8,128)(2,1)}, bf16[1024,128]{1,0:T(8,128)(2,1)S(1)}, u32[]{:S(2)}, u32[]{:S(2)}) %collective-permute-start.78) | collective-permute-done | bytes 262176 | tf_op jit(solution)/shard_map/ppermute | solution.py:34
  590.3 32.1 %collective-permute-done.82.refs_10_ = bf16[1024,128]{1,0:T(8,128)(2,1)} collective-permute-done((bf16[1024,128]{1,0:T(8,128)(2,1)}, bf16[1024,128]{1,0:T(8,128)(2,1)}, u32[]{:S(2)}, u32[]{:S(2)}) %collective-permute-start.82) | collective-permute-done | bytes 262176 | tf_op jit(solution)/shard_map/ppermute | solution.py:34
  627.3 20.4 %collective-permute-done.64.refs_7_ = bf16[1280,128]{1,0:T(8,128)(2,1)S(1)} collective-permute-done((bf16[1280,128]{1,0:T(8,128)(2,1)S(1)}, bf16[1280,128]{1,0:T(8,128)(2,1)S(1)}, u32[]{:S(2)}, u32[]{:S(2)}) %collective-permute-start.64) | collective-permute-done | bytes 327712 | tf_op jit(solution)/shard_map/ppermute | solution.py:34
  669.5 22.3 %collective-permute-done.71.refs_14_ = bf16[1280,128]{1,0:T(8,128)(2,1)} collective-permute-done((bf16[1280,128]{1,0:T(8,128)(2,1)}, bf16[1280,128]{1,0:T(8,128)(2,1)}, u32[]{:S(2)}, u32[]{:S(2)}) %collective-permute-start.71) | collective-permute-done | bytes 327712 | tf_op jit(solution)/shard_map/ppermute | solution.py:34
  704.4 12.1 %collective-permute-done.75.refs_18_ = bf16[1280,128]{1,0:T(8,128)(2,1)} collective-permute-done((bf16[1280,128]{1,0:T(8,128)(2,1)}, bf16[1280,128]{1,0:T(8,128)(2,1)}, u32[]{:S(2)}, u32[]{:S(2)}) %collective-permute-start.75) | collective-permute-done | bytes 327712 | tf_op jit(solution)/shard_map/ppermute | solution.py:34
  716.5 26.7 %shard_map.56 = (bf16[512,128]{1,0:T(8,128)(2,1)}, bf16[512,128]{1,0:T(8,128)(2,1)}, bf16[512,128]{1,0:T(8,128)(2,1)}, bf16[512,128]{1,0:T(8,128)(2,1)}, bf16[51...) custom-call(s32[1]{0:T(128)} %bitcast.2.me_ref, ...), custom_call_target="tpu_custom_call" | custom-call | flops 6039797760 | bytes 50757632 | tf_op jit(solution)/shard_map/pallas_call | solution.py:135
  749.2 25.6 %shard_map.57 = (bf16[384,128]{1,0:T(8,128)(2,1)}, bf16[384,128]{1,0:T(8,128)(2,1)}, bf16[384,128]{1,0:T(8,128)(2,1)}, bf16[384,128]{1,0:T(8,128)(2,1)}, bf16[38...) custom-call(s32[1]{0:T(128)} %bitcast.2.me_ref, ...), custom_call_target="tpu_custom_call" | custom-call | flops 4529848320 | bytes 49864704 | tf_op jit(solution)/shard_map/pallas_call | solution.py:135
  781.2 12.0 %shard_map.58.refs_19_ = f32[2048,5760]{1,0:T(8,128)} custom-call(bf16[8,2048,128]{2,1,0:T(8,128)(2,1)} %bitcast.refs_0_, bf16[8,2048,128]{2,1,0:T(8,128)(2,1)} %bitcast.1.refs_1_, f32[2048,256]{1,0:T(8,128)} %shard_map.48.refs_2_, bf16[768,128]{1,0:T(8,128)(2,1)} %get-tuple-element.547.refs_3_, bf16[768,128]{1,0:T(8,128)(2,1)} %copy-done.59, ...), custom_call_target="tpu_custom_call" | custom-call | flops 6442450944 | bytes 17825792 | tf_op jit(solution)/shard_map/pallas_call | solution.py:196
  799.7 14.0 %shard_map.59.refs_19_ = f32[2048,5760]{1,0:T(8,128)} custom-call(bf16[8,2048,128]{2,1,0:T(8,128)(2,1)} %bitcast.refs_0_, bf16[8,2048,128]{2,1,0:T(8,128)(2,1)} %bitcast.1.refs_1_, f32[2048,256]{1,0:T(8,128)} %shard_map.48.refs_2_, bf16[1024,128]{1,0:T(8,128)(2,1)} %get-tuple-element.531.refs_3_, ...), custom_call_target="tpu_custom_call", output_to_operand_aliasing={{}: (19, {})} | custom-call | flops 8589934592 | bytes 20971520 | tf_op jit(solution)/shard_map/pallas_call | solution.py:196
  839.5 16.6 %shard_map.61.refs_19_ = f32[2048,5760]{1,0:T(8,128)} custom-call(bf16[8,2048,128]{2,1,0:T(8,128)(2,1)} %bitcast.refs_0_, bf16[8,2048,128]{2,1,0:T(8,128)(2,1)} %bitcast.1.refs_1_, f32[2048,256]{1,0:T(8,128)} %shard_map.48.refs_2_, bf16[1280,128]{1,0:T(8,128)(2,1)} %get-tuple-element.499.refs_3_, ...), custom_call_target="tpu_custom_call", output_to_operand_aliasing={{}: (19, {})} | custom-call | flops 10737418240 | bytes 24117248 | tf_op jit(solution)/shard_map/pallas_call | solution.py:196
  863.5 14.0 %shard_map.62.refs_19_ = f32[2048,5760]{1,0:T(8,128)} custom-call(bf16[8,2048,128]{2,1,0:T(8,128)(2,1)} %bitcast.refs_0_, bf16[8,2048,128]{2,1,0:T(8,128)(2,1)} %bitcast.1.refs_1_, f32[2048,256]{1,0:T(8,128)} %shard_map.48.refs_2_, bf16[1024,128]{1,0:T(8,128)(2,1)} %get-tuple-element.483.refs_3_, ...), custom_call_target="tpu_custom_call", output_to_operand_aliasing={{}: (19, {})} | custom-call | flops 8589934592 | bytes 20971520 | tf_op jit(solution)/shard_map/pallas_call | solution.py:196
  (551 shorter events, 350.6 us)
Async XLA Ops:
  28.3 42.9 %collective-permute-start.4 = (bf16[192,1664]{1,0:T(8,128)(2,1)}, bf16[192,1664]{1,0:T(8,128)(2,1)S(1)}, u32[]{:S(2)}, u32[]{:S(2)}) collective-permute-start(bf16[192,1664]{1,0:T(8,128)(2,1)} %get-tuple-element.284), channel_id=1, source_target_pairs={{0,16},{2,18},{4,20},{6,22},{8,24},{10,26},{12,28},{14,30},{16,0},... | collective-permute-start | bytes 1916936 | tf_op jit(solution)/shard_map/ppermute | solution.py:34
  73.3 50.1 %collective-permute-start.5 = (bf16[384,1664]{1,0:T(8,128)(2,1)}, bf16[384,1664]{1,0:T(8,128)(2,1)}, u32[]{:S(2)}, u32[]{:S(2)}) collective-permute-start(bf16[384,1664]{1,0:T(8,128)(2,1)} %pad_maximum_fusion.4), channel_id=1, source_target_pairs={{0,8},{2,10},{4,12},{6,14},{8,0},{10,2},{12,4},{14,6},{16,24},{18,... | collective-permute-start | bytes 3833864 | tf_op jit(solution)/shard_map/ppermute | solution.py:34
  75.3 40.4 %collective-permute-start = (bf16[2048,128]{1,0:T(8,128)(2,1)}, bf16[2048,128]{1,0:T(8,128)(2,1)}, u32[]{:S(2)}, u32[]{:S(2)}) collective-permute-start(bf16[2048,128]{1,0:T(8,128)(2,1)} %shard_map.46), channel_id=1, source_target_pairs={{0,16},{2,18},{4,20},{6,22},{8,24},{10,26},{12,28},{14,30},{16,0},... | collective-permute-start | bytes 1572872 | tf_op jit(solution)/shard_map/ppermute | solution.py:34
  117.8 48.7 %collective-permute-start.1 = (bf16[4096,128]{1,0:T(8,128)(2,1)}, bf16[4096,128]{1,0:T(8,128)(2,1)}, u32[]{:S(2)}, u32[]{:S(2)}) collective-permute-start(bf16[4096,128]{1,0:T(8,128)(2,1)} %pad_maximum_fusion.6), channel_id=1, source_target_pairs={{0,8},{2,10},{4,12},{6,14},{8,0},{10,2},{12,4},{14,6},{16,24},{18,... | collective-permute-start | bytes 3145736 | tf_op jit(solution)/shard_map/ppermute | solution.py:34
  126.4 127.5 %collective-permute-start.6 = (bf16[768,1664]{1,0:T(8,128)(2,1)}, bf16[768,1664]{1,0:T(8,128)(2,1)}, u32[]{:S(2)}, u32[]{:S(2)}) collective-permute-start(bf16[768,1664]{1,0:T(8,128)(2,1)} %pad_maximum_fusion.1), channel_id=1, source_target_pairs={{0,4},{2,6},{4,0},{6,2},{8,12},{10,14},{12,8},{14,10},{16,20},{18,... | collective-permute-start | bytes 7667720 | tf_op jit(solution)/shard_map/ppermute | solution.py:34
  130.2 146.5 %collective-permute-start.14 = (bf16[1536,896]{1,0:T(8,128)(2,1)S(1)}, bf16[1536,896]{1,0:T(8,128)(2,1)}, u32[]{:S(2)}, u32[]{:S(2)}) collective-permute-start(bf16[1536,896]{1,0:T(8,128)(2,1)S(1)} %constant_dynamic-update-slice_fusion.4.refs_0_), channel_id=1, source_target_pairs={{0,2},{2,0},{4,6},{6,4},{8,10},{10,8},{12,14},{14,12},{16,18},{18,... | collective-permute-start | bytes 8257544 | tf_op jit(solution)/shard_map/ppermute | solution.py:34
  175.0 136.7 %collective-permute-start.2 = (bf16[8192,128]{1,0:T(8,128)(2,1)}, bf16[8192,128]{1,0:T(8,128)(2,1)}, u32[]{:S(2)}, u32[]{:S(2)}) collective-permute-start(bf16[8192,128]{1,0:T(8,128)(2,1)} %pad_maximum_fusion.2), channel_id=1, source_target_pairs={{0,4},{2,6},{4,0},{6,2},{8,12},{10,14},{12,8},{14,10},{16,20},{18,... | collective-permute-start | bytes 6291464 | tf_op jit(solution)/shard_map/ppermute | solution.py:34
  176.2 60.9 %collective-permute-start.19 = (bf16[768,128]{1,0:T(8,128)(2,1)S(1)}, bf16[768,128]{1,0:T(8,128)(2,1)}, u32[]{:S(2)}, u32[]{:S(2)}) collective-permute-start(bf16[768,128]{1,0:T(8,128)(2,1)S(1)} %copy-done.122), channel_id=1, source_target_pairs={{0,4},{2,6},{4,0},{6,2},{8,12},{10,14},{12,8},{14,10},{16,20},{18,... | collective-permute-start | bytes 589832 | tf_op jit(solution)/shard_map/ppermute | solution.py:34
  183.2 57.0 %collective-permute-start.20 = (bf16[768,128]{1,0:T(8,128)(2,1)S(1)}, bf16[768,128]{1,0:T(8,128)(2,1)}, u32[]{:S(2)}, u32[]{:S(2)}) collective-permute-start(bf16[768,128]{1,0:T(8,128)(2,1)S(1)} %copy-done.121), channel_id=1, source_target_pairs={{0,20},{2,22},{4,16},{6,18},{8,28},{10,30},{12,24},{14,26},{16,4},... | collective-permute-start | bytes 589832 | tf_op jit(solution)/shard_map/ppermute | solution.py:34
  258.7 209.2 %collective-permute-start.7 = (bf16[1536,1664]{1,0:T(8,128)(2,1)}, bf16[1536,1664]{1,0:T(8,128)(2,1)}, u32[]{:S(2)}, u32[]{:S(2)}) collective-permute-start(bf16[1536,1664]{1,0:T(8,128)(2,1)} %constant_dynamic-update-slice_fusion.refs_0_), channel_id=1, source_target_pairs={{0,2},{2,0},{4,6},{6,4},{8,10},{10,8},{12,14},{14,12},{16,18},{18,... | collective-permute-start | bytes 15335432 | tf_op jit(solution)/shard_map/ppermute | solution.py:34
  310.6 45.7 %collective-permute-start.48 = (bf16[768,128]{1,0:T(8,128)(2,1)}, bf16[768,128]{1,0:T(8,128)(2,1)S(1)}, u32[]{:S(2)}, u32[]{:S(2)}) collective-permute-start(bf16[768,128]{1,0:T(8,128)(2,1)} %get-tuple-element.372), channel_id=1, source_target_pairs={{0,24},{2,26},{4,28},{6,30},{8,16},{10,18},{12,20},{14,22},{16,8},... | collective-permute-start | bytes 589832 | tf_op jit(solution)/shard_map/ppermute | solution.py:34
  311.7 46.2 %collective-permute-start.49 = (bf16[768,128]{1,0:T(8,128)(2,1)}, bf16[768,128]{1,0:T(8,128)(2,1)S(1)}, u32[]{:S(2)}, u32[]{:S(2)}) collective-permute-start(bf16[768,128]{1,0:T(8,128)(2,1)} %get-tuple-element.373), channel_id=1, source_target_pairs={{0,4},{2,6},{4,0},{6,2},{8,12},{10,14},{12,8},{14,10},{16,20},{18,... | collective-permute-start | bytes 589832 | tf_op jit(solution)/shard_map/ppermute | solution.py:34
  318.7 39.2 %collective-permute-start.50 = (bf16[768,128]{1,0:T(8,128)(2,1)}, bf16[768,128]{1,0:T(8,128)(2,1)S(1)}, u32[]{:S(2)}, u32[]{:S(2)}) collective-permute-start(bf16[768,128]{1,0:T(8,128)(2,1)} %get-tuple-element.374), channel_id=1, source_target_pairs={{0,20},{2,22},{4,16},{6,18},{8,28},{10,30},{12,24},{14,26},{16,4},... | collective-permute-start | bytes 589832 | tf_op jit(solution)/shard_map/ppermute | solution.py:34
  455.7 322.5 %collective-permute-start.3 = (bf16[16384,128]{1,0:T(8,128)(2,1)}, bf16[16384,128]{1,0:T(8,128)(2,1)}, u32[]{:S(2)}, u32[]{:S(2)}) collective-permute-start(bf16[16384,128]{1,0:T(8,128)(2,1)} %pad_maximum_fusion), channel_id=1, source_target_pairs={{0,2},{2,0},{4,6},{6,4},{8,10},{10,8},{12,14},{14,12},{16,18},{18,... | collective-permute-start | bytes 12582920 | tf_op jit(solution)/shard_map/ppermute | solution.py:34
  456.4 47.9 %collective-permute-start.53 = (bf16[768,128]{1,0:T(8,128)(2,1)}, bf16[768,128]{1,0:T(8,128)(2,1)S(1)}, u32[]{:S(2)}, u32[]{:S(2)}) collective-permute-start(bf16[768,128]{1,0:T(8,128)(2,1)} %get-tuple-element.377), channel_id=1, source_target_pairs={{0,2},{2,0},{4,6},{6,4},{8,10},{10,8},{12,14},{14,12},{16,18},{18,... | collective-permute-start | bytes 589832 | tf_op jit(solution)/shard_map/ppermute | solution.py:34
  456.6 49.3 %collective-permute-start.54 = (bf16[768,128]{1,0:T(8,128)(2,1)}, bf16[768,128]{1,0:T(8,128)(2,1)S(1)}, u32[]{:S(2)}, u32[]{:S(2)}) collective-permute-start(bf16[768,128]{1,0:T(8,128)(2,1)} %get-tuple-element.378), channel_id=1, source_target_pairs={{0,18},{2,16},{4,22},{6,20},{8,26},{10,24},{12,30},{14,28},{16,2},... | collective-permute-start | bytes 589832 | tf_op jit(solution)/shard_map/ppermute | solution.py:34
  467.9 41.8 %collective-permute-start.55 = (bf16[768,128]{1,0:T(8,128)(2,1)}, bf16[768,128]{1,0:T(8,128)(2,1)S(1)}, u32[]{:S(2)}, u32[]{:S(2)}) collective-permute-start(bf16[768,128]{1,0:T(8,128)(2,1)} %get-tuple-element.379), channel_id=1, source_target_pairs={{0,10},{2,8},{4,14},{6,12},{8,2},{10,0},{12,6},{14,4},{16,26},{18,... | collective-permute-start | bytes 589832 | tf_op jit(solution)/shard_map/ppermute | solution.py:34
  467.9 41.8 %collective-permute-start.56 = (bf16[768,128]{1,0:T(8,128)(2,1)}, bf16[768,128]{1,0:T(8,128)(2,1)S(1)}, u32[]{:S(2)}, u32[]{:S(2)}) collective-permute-start(bf16[768,128]{1,0:T(8,128)(2,1)} %get-tuple-element.380), channel_id=1, source_target_pairs={{0,26},{2,24},{4,30},{6,28},{8,18},{10,16},{12,22},{14,20},{16,10}... | collective-permute-start | bytes 589832 | tf_op jit(solution)/shard_map/ppermute | solution.py:34
  504.3 38.8 %collective-permute-start.57 = (bf16[768,128]{1,0:T(8,128)(2,1)}, bf16[768,128]{1,0:T(8,128)(2,1)S(1)}, u32[]{:S(2)}, u32[]{:S(2)}) collective-permute-start(bf16[768,128]{1,0:T(8,128)(2,1)} %get-tuple-element.381), channel_id=1, source_target_pairs={{0,6},{2,4},{4,2},{6,0},{8,14},{10,12},{12,10},{14,8},{16,22},{18,... | collective-permute-start | bytes 589832 | tf_op jit(solution)/shard_map/ppermute | solution.py:34
  576.9 46.2 %collective-permute-start.61 = (bf16[1280,128]{1,0:T(8,128)(2,1)S(1)}, bf16[1280,128]{1,0:T(8,128)(2,1)S(1)}, u32[]{:S(2)}, u32[]{:S(2)}) collective-permute-start(bf16[1280,128]{1,0:T(8,128)(2,1)S(1)} %copy-done.105), channel_id=1, source_target_pairs={{0,16},{2,18},{4,20},{6,22},{8,24},{10,26},{12,28},{14,30},{16,0},... | collective-permute-start | bytes 983048 | tf_op jit(solution)/shard_map/ppermute | solution.py:34
  576.9 46.3 %collective-permute-start.62 = (bf16[1280,128]{1,0:T(8,128)(2,1)S(1)}, bf16[1280,128]{1,0:T(8,128)(2,1)S(1)}, u32[]{:S(2)}, u32[]{:S(2)}) collective-permute-start(bf16[1280,128]{1,0:T(8,128)(2,1)S(1)} %copy-done.104), channel_id=1, source_target_pairs={{0,8},{2,10},{4,12},{6,14},{8,0},{10,2},{12,4},{14,6},{16,24},{18,... | collective-permute-start | bytes 983048 | tf_op jit(solution)/shard_map/ppermute | solution.py:34
  698.7 44.6 %collective-permute-start.83 = (bf16[1024,128]{1,0:T(8,128)(2,1)}, bf16[1024,128]{1,0:T(8,128)(2,1)S(1)}, u32[]{:S(2)}, u32[]{:S(2)}) collective-permute-start(bf16[1024,128]{1,0:T(8,128)(2,1)} %get-tuple-element.443), channel_id=1, source_target_pairs={{0,2},{2,0},{4,6},{6,4},{8,10},{10,8},{12,14},{14,12},{16,18},{18,... | collective-permute-start | bytes 786440 | tf_op jit(solution)/shard_map/ppermute | solution.py:34
  700.7 44.8 %collective-permute-start.84 = (bf16[1024,128]{1,0:T(8,128)(2,1)}, bf16[1024,128]{1,0:T(8,128)(2,1)S(1)}, u32[]{:S(2)}, u32[]{:S(2)}) collective-permute-start(bf16[1024,128]{1,0:T(8,128)(2,1)} %get-tuple-element.444), channel_id=1, source_target_pairs={{0,18},{2,16},{4,22},{6,20},{8,26},{10,24},{12,30},{14,28},{16,2},... | collective-permute-start | bytes 786440 | tf_op jit(solution)/shard_map/ppermute | solution.py:34
  704.4 41.1 %collective-permute-start.85 = (bf16[1024,128]{1,0:T(8,128)(2,1)}, bf16[1024,128]{1,0:T(8,128)(2,1)S(1)}, u32[]{:S(2)}, u32[]{:S(2)}) collective-permute-start(bf16[1024,128]{1,0:T(8,128)(2,1)} %get-tuple-element.445), channel_id=1, source_target_pairs={{0,10},{2,8},{4,14},{6,12},{8,2},{10,0},{12,6},{14,4},{16,26},{18,... | collective-permute-start | bytes 786440 | tf_op jit(solution)/shard_map/ppermute | solution.py:34
  (245 other events, 7245.7 us)

commit v4 on v3

--- a/solution.py
+++ b/solution.py
@@ -107,7 +107,13 @@
             both = jnp.concatenate([jnp.where(even, own, other), jnp.where(even, other, own)])
             start = pl.multiple_of((me_ref[0] ^ offset) // 2 * (2 * part), 8)
             stage[pl.ds(start, 2 * part), :] = both
-        basis_t[...] = stage[...].T.astype(jnp.bfloat16)
+
+        def turned(tile, carry):
+            lanes = pl.ds(pl.multiple_of(tile * LANES, LANES), LANES)
+            basis_t[lanes, :] = stage[:, lanes].T.astype(jnp.bfloat16)
+            return carry
+
+        lax.fori_loop(0, stage.shape[1] // LANES, turned, 0)
 
     pair[:, :LANES] = grad_ref[0].astype(jnp.bfloat16)
     pair[:, LANES:] = grad_ref[1].astype(jnp.bfloat16)
@@ -231,7 +237,8 @@
     middle, late = arrange(in_basis, devices, spans[1:])
     early = spread(early)
     gathered = [early, spread(middle, early[0]), spread(late)]
-    basis = [block.reshape(devices // 2, -1, LANES) for block in spread(turn(out_basis))]
+    out_basis = turn(out_basis)
+    basis = [block.reshape(devices // 2, -1, LANES) for block in spread(out_basis)]
     scale = eigen(eigen_seeds)
     scale = turn(scale)
     grad = gradients.transpose(1, 2, 0)

time: 918 us -> 918 us (level)
  no operation moved by 1% of the time
where the time goes in v4:
time: 918 us; the launch traced here: 907 us
  waiting for transfers between devices  381 us (42%)
  Pallas kernels  317 us (35%)
  starting transfers between devices  168 us (18%)
  other arithmetic  22.9 us (2%)
  local copies, waits for them, and re-layouts  16.2 us (2%)
    ppermute x121, waiting for transfers between devices, exchange(): lax.ppermute(block, 'rows', [(source, source ^ flip) for source in range(...  381 us
    pallas_call x7, Pallas kernels, rotate(): pl.pallas_call(functools.partial(rotate_kernel, columns, part, grads, ord...  215 us
    ppermute x121, starting transfers between devices, exchange(): lax.ppermute(block, 'rows', [(source, source ^ flip) for source in range(...  168 us
    pallas_call x7, Pallas kernels, finish(): pl.pallas_call(functools.partial(finish_kernel, begin, grads, devices), g...  86.9 us
    concatenate x10, other arithmetic, spread(): block = jnp.concatenate([block, other])  22.9 us
  transfers between devices with their start and end apart: 121, of which 32 were waited for; matrix products, arithmetic and copies ran while one was open for 4% of the time, Pallas kernels for 34%

profile of v4, /device:TPU:11, one launch (start us, length us, event | category | flops | bytes accessed | tf_op | source)
XLA Modules:
  0.0 906.6 jit_solution(4728847083889518714)
XLA Ops:
  36.3 21.2 %collective-permute-done.8 = bf16[192,896]{1,0:T(8,128)(2,1)S(1)} collective-permute-done((bf16[192,896]{1,0:T(8,128)(2,1)}, bf16[192,896]{1,0:T(8,128)(2,1)S(1)}, u32[]{:S(2)}, u32[]{:S(2)}) %collective-permute-start.8) | collective-permute-done | bytes 344096 | tf_op jit(solution)/shard_map/ppermute | solution.py:34
  58.7 12.5 %collective-permute-done.4 = bf16[192,1664]{1,0:T(8,128)(2,1)S(1)} collective-permute-done((bf16[192,1664]{1,0:T(8,128)(2,1)}, bf16[192,1664]{1,0:T(8,128)(2,1)S(1)}, u32[]{:S(2)}, u32[]{:S(2)}) %collective-permute-start.4) | collective-permute-done | bytes 639008 | tf_op jit(solution)/shard_map/ppermute | solution.py:34
  78.3 17.6 %collective-permute-done.12 = bf16[384,896]{1,0:T(8,128)(2,1)S(1)} collective-permute-done((bf16[384,896]{1,0:T(8,128)(2,1)S(1)}, bf16[384,896]{1,0:T(8,128)(2,1)S(1)}, u32[]{:S(2)}, u32[]{:S(2)}) %collective-permute-start.12) | collective-permute-done | bytes 688160 | tf_op jit(solution)/shard_map/ppermute | solution.py:34
  101.2 14.5 %collective-permute-done = bf16[2048,128]{1,0:T(8,128)(2,1)} collective-permute-done((bf16[2048,128]{1,0:T(8,128)(2,1)}, bf16[2048,128]{1,0:T(8,128)(2,1)}, u32[]{:S(2)}, u32[]{:S(2)}) %collective-permute-start) | collective-permute-done | bytes 524320 | tf_op jit(solution)/shard_map/ppermute | solution.py:34
  132.0 30.2 %shard_map.52 = (bf16[768,128]{1,0:T(8,128)(2,1)}, bf16[768,128]{1,0:T(8,128)(2,1)}, bf16[768,128]{1,0:T(8,128)(2,1)}, bf16[768,128]{1,0:T(8,128)(2,1)}, bf16[76...) custom-call(s32[1]{0:T(128)} %bitcast.2.me_ref, ...), custom_call_target="tpu_custom_call" | custom-call | flops 9059696640 | bytes 52543488 | tf_op jit(solution)/shard_map/pallas_call | solution.py:141
  184.3 52.8 %collective-permute-done.19.refs_7_ = bf16[768,128]{1,0:T(8,128)(2,1)} collective-permute-done((bf16[768,128]{1,0:T(8,128)(2,1)S(1)}, bf16[768,128]{1,0:T(8,128)(2,1)}, u32[]{:S(2)}, u32[]{:S(2)}) %collective-permute-start.19) | collective-permute-done | bytes 196640 | tf_op jit(solution)/shard_map/ppermute | solution.py:34
  279.2 29.8 %shard_map.51 = (bf16[768,128]{1,0:T(8,128)(2,1)}, bf16[768,128]{1,0:T(8,128)(2,1)}, bf16[768,128]{1,0:T(8,128)(2,1)}, bf16[768,128]{1,0:T(8,128)(2,1)}, bf16[76...) custom-call(s32[1]{0:T(128)} %bitcast.2.me_ref, ...), custom_call_target="tpu_custom_call" | custom-call | flops 9059696640 | bytes 52543488 | tf_op jit(solution)/shard_map/pallas_call | solution.py:141
  323.1 33.1 %shard_map.54 = (bf16[1024,128]{1,0:T(8,128)(2,1)}, bf16[1024,128]{1,0:T(8,128)(2,1)}, bf16[1024,128]{1,0:T(8,128)(2,1)}, bf16[1024,128]{1,0:T(8,128)(2,1)}, bf1...) custom-call(s32[1]{0:T(128)} %bitcast.2.me_ref, ...), custom_call_target="tpu_custom_call" | custom-call | flops 12079595520 | bytes 54329344 | tf_op jit(solution)/shard_map/pallas_call | solution.py:141
  361.0 29.9 %collective-permute-done.52.refs_10_ = bf16[768,128]{1,0:T(8,128)(2,1)S(1)} collective-permute-done((bf16[768,128]{1,0:T(8,128)(2,1)S(1)}, bf16[768,128]{1,0:T(8,128)(2,1)S(1)}, u32[]{:S(2)}, u32[]{:S(2)}) %collective-permute-start.52) | collective-permute-done | bytes 196640 | tf_op jit(solution)/shard_map/ppermute | solution.py:34
  396.4 16.7 %collective-permute-done.34.refs_7_ = bf16[1024,128]{1,0:T(8,128)(2,1)S(1)} collective-permute-done((bf16[1024,128]{1,0:T(8,128)(2,1)}, bf16[1024,128]{1,0:T(8,128)(2,1)S(1)}, u32[]{:S(2)}, u32[]{:S(2)}) %collective-permute-start.34) | collective-permute-done | bytes 262176 | tf_op jit(solution)/shard_map/ppermute | solution.py:34
  430.9 15.3 %collective-permute-done.41.refs_14_ = bf16[1024,128]{1,0:T(8,128)(2,1)S(1)} collective-permute-done((bf16[1024,128]{1,0:T(8,128)(2,1)}, bf16[1024,128]{1,0:T(8,128)(2,1)S(1)}, u32[]{:S(2)}, u32[]{:S(2)}) %collective-permute-start.41) | collective-permute-done | bytes 262176 | tf_op jit(solution)/shard_map/ppermute | solution.py:34
  468.0 36.5 %shard_map.53 = (bf16[1280,128]{1,0:T(8,128)(2,1)}, bf16[1280,128]{1,0:T(8,128)(2,1)}, bf16[1280,128]{1,0:T(8,128)(2,1)}, bf16[1280,128]{1,0:T(8,128)(2,1)}, bf1...) custom-call(s32[1]{0:T(128)} %bitcast.2.me_ref, ...), custom_call_target="tpu_custom_call" | custom-call | flops 15099494400 | bytes 56115200 | tf_op jit(solution)/shard_map/pallas_call | solution.py:141
  510.2 33.3 %shard_map.55 = (bf16[1024,128]{1,0:T(8,128)(2,1)}, bf16[1024,128]{1,0:T(8,128)(2,1)}, bf16[1024,128]{1,0:T(8,128)(2,1)}, bf16[1024,128]{1,0:T(8,128)(2,1)}, bf1...) custom-call(s32[1]{0:T(128)} %bitcast.2.me_ref, ...), custom_call_target="tpu_custom_call" | custom-call | flops 12079595520 | bytes 54329344 | tf_op jit(solution)/shard_map/pallas_call | solution.py:141
  562.8 14.4 %collective-permute-done.78.refs_6_ = bf16[1024,128]{1,0:T(8,128)(2,1)S(1)} collective-permute-done((bf16[1024,128]{1,0:T(8,128)(2,1)}, bf16[1024,128]{1,0:T(8,128)(2,1)S(1)}, u32[]{:S(2)}, u32[]{:S(2)}) %collective-permute-start.78) | collective-permute-done | bytes 262176 | tf_op jit(solution)/shard_map/ppermute | solution.py:34
  590.7 32.1 %collective-permute-done.82.refs_10_ = bf16[1024,128]{1,0:T(8,128)(2,1)} collective-permute-done((bf16[1024,128]{1,0:T(8,128)(2,1)}, bf16[1024,128]{1,0:T(8,128)(2,1)}, u32[]{:S(2)}, u32[]{:S(2)}) %collective-permute-start.82) | collective-permute-done | bytes 262176 | tf_op jit(solution)/shard_map/ppermute | solution.py:34
  627.7 20.4 %collective-permute-done.64.refs_7_ = bf16[1280,128]{1,0:T(8,128)(2,1)S(1)} collective-permute-done((bf16[1280,128]{1,0:T(8,128)(2,1)S(1)}, bf16[1280,128]{1,0:T(8,128)(2,1)S(1)}, u32[]{:S(2)}, u32[]{:S(2)}) %collective-permute-start.64) | collective-permute-done | bytes 327712 | tf_op jit(solution)/shard_map/ppermute | solution.py:34
  669.9 22.4 %collective-permute-done.71.refs_14_ = bf16[1280,128]{1,0:T(8,128)(2,1)} collective-permute-done((bf16[1280,128]{1,0:T(8,128)(2,1)}, bf16[1280,128]{1,0:T(8,128)(2,1)}, u32[]{:S(2)}, u32[]{:S(2)}) %collective-permute-start.71) | collective-permute-done | bytes 327712 | tf_op jit(solution)/shard_map/ppermute | solution.py:34
  704.8 12.1 %collective-permute-done.75.refs_18_ = bf16[1280,128]{1,0:T(8,128)(2,1)} collective-permute-done((bf16[1280,128]{1,0:T(8,128)(2,1)}, bf16[1280,128]{1,0:T(8,128)(2,1)}, u32[]{:S(2)}, u32[]{:S(2)}) %collective-permute-start.75) | collective-permute-done | bytes 327712 | tf_op jit(solution)/shard_map/ppermute | solution.py:34
  716.9 26.8 %shard_map.56 = (bf16[512,128]{1,0:T(8,128)(2,1)}, bf16[512,128]{1,0:T(8,128)(2,1)}, bf16[512,128]{1,0:T(8,128)(2,1)}, bf16[512,128]{1,0:T(8,128)(2,1)}, bf16[51...) custom-call(s32[1]{0:T(128)} %bitcast.2.me_ref, ...), custom_call_target="tpu_custom_call" | custom-call | flops 6039797760 | bytes 50757632 | tf_op jit(solution)/shard_map/pallas_call | solution.py:141
  749.6 25.7 %shard_map.57 = (bf16[384,128]{1,0:T(8,128)(2,1)}, bf16[384,128]{1,0:T(8,128)(2,1)}, bf16[384,128]{1,0:T(8,128)(2,1)}, bf16[384,128]{1,0:T(8,128)(2,1)}, bf16[38...) custom-call(s32[1]{0:T(128)} %bitcast.2.me_ref, ...), custom_call_target="tpu_custom_call" | custom-call | flops 4529848320 | bytes 49864704 | tf_op jit(solution)/shard_map/pallas_call | solution.py:141
  800.0 14.0 %shard_map.59.refs_19_ = f32[2048,5760]{1,0:T(8,128)} custom-call(bf16[8,2048,128]{2,1,0:T(8,128)(2,1)} %bitcast.refs_0_, bf16[8,2048,128]{2,1,0:T(8,128)(2,1)} %bitcast.1.refs_1_, f32[2048,256]{1,0:T(8,128)} %shard_map.48.refs_2_, bf16[1024,128]{1,0:T(8,128)(2,1)} %get-tuple-element.531.refs_3_, ...), custom_call_target="tpu_custom_call", output_to_operand_aliasing={{}: (19, {})} | custom-call | flops 8589934592 | bytes 20971520 | tf_op jit(solution)/shard_map/pallas_call | solution.py:202
  821.2 11.9 %shard_map.60.refs_19_ = f32[2048,5760]{1,0:T(8,128)} custom-call(bf16[8,2048,128]{2,1,0:T(8,128)(2,1)} %bitcast.refs_0_, bf16[8,2048,128]{2,1,0:T(8,128)(2,1)} %bitcast.1.refs_1_, f32[2048,256]{1,0:T(8,128)} %shard_map.48.refs_2_, bf16[768,128]{1,0:T(8,128)(2,1)} %get-tuple-element.515.refs_3_, ...), custom_call_target="tpu_custom_call", output_to_operand_aliasing={{}: (19, {})} | custom-call | flops 6442450944 | bytes 17825792 | tf_op jit(solution)/shard_map/pallas_call | solution.py:202
  840.0 16.6 %shard_map.61.refs_19_ = f32[2048,5760]{1,0:T(8,128)} custom-call(bf16[8,2048,128]{2,1,0:T(8,128)(2,1)} %bitcast.refs_0_, bf16[8,2048,128]{2,1,0:T(8,128)(2,1)} %bitcast.1.refs_1_, f32[2048,256]{1,0:T(8,128)} %shard_map.48.refs_2_, bf16[1280,128]{1,0:T(8,128)(2,1)} %get-tuple-element.499.refs_3_, ...), custom_call_target="tpu_custom_call", output_to_operand_aliasing={{}: (19, {})} | custom-call | flops 10737418240 | bytes 24117248 | tf_op jit(solution)/shard_map/pallas_call | solution.py:202
  864.1 14.0 %shard_map.62.refs_19_ = f32[2048,5760]{1,0:T(8,128)} custom-call(bf16[8,2048,128]{2,1,0:T(8,128)(2,1)} %bitcast.refs_0_, bf16[8,2048,128]{2,1,0:T(8,128)(2,1)} %bitcast.1.refs_1_, f32[2048,256]{1,0:T(8,128)} %shard_map.48.refs_2_, bf16[1024,128]{1,0:T(8,128)(2,1)} %get-tuple-element.483.refs_3_, ...), custom_call_target="tpu_custom_call", output_to_operand_aliasing={{}: (19, {})} | custom-call | flops 8589934592 | bytes 20971520 | tf_op jit(solution)/shard_map/pallas_call | solution.py:202
  (551 shorter events, 350.7 us)
Async XLA Ops:
  28.3 42.9 %collective-permute-start.4 = (bf16[192,1664]{1,0:T(8,128)(2,1)}, bf16[192,1664]{1,0:T(8,128)(2,1)S(1)}, u32[]{:S(2)}, u32[]{:S(2)}) collective-permute-start(bf16[192,1664]{1,0:T(8,128)(2,1)} %get-tuple-element.284), channel_id=1, source_target_pairs={{0,16},{2,18},{4,20},{6,22},{8,24},{10,26},{12,28},{14,30},{16,0},... | collective-permute-start | bytes 1916936 | tf_op jit(solution)/shard_map/ppermute | solution.py:34
  73.3 50.1 %collective-permute-start.5 = (bf16[384,1664]{1,0:T(8,128)(2,1)}, bf16[384,1664]{1,0:T(8,128)(2,1)}, u32[]{:S(2)}, u32[]{:S(2)}) collective-permute-start(bf16[384,1664]{1,0:T(8,128)(2,1)} %pad_maximum_fusion.4), channel_id=1, source_target_pairs={{0,8},{2,10},{4,12},{6,14},{8,0},{10,2},{12,4},{14,6},{16,24},{18,... | collective-permute-start | bytes 3833864 | tf_op jit(solution)/shard_map/ppermute | solution.py:34
  75.3 40.4 %collective-permute-start = (bf16[2048,128]{1,0:T(8,128)(2,1)}, bf16[2048,128]{1,0:T(8,128)(2,1)}, u32[]{:S(2)}, u32[]{:S(2)}) collective-permute-start(bf16[2048,128]{1,0:T(8,128)(2,1)} %shard_map.46), channel_id=1, source_target_pairs={{0,16},{2,18},{4,20},{6,22},{8,24},{10,26},{12,28},{14,30},{16,0},... | collective-permute-start | bytes 1572872 | tf_op jit(solution)/shard_map/ppermute | solution.py:34
  117.8 48.8 %collective-permute-start.1 = (bf16[4096,128]{1,0:T(8,128)(2,1)}, bf16[4096,128]{1,0:T(8,128)(2,1)}, u32[]{:S(2)}, u32[]{:S(2)}) collective-permute-start(bf16[4096,128]{1,0:T(8,128)(2,1)} %pad_maximum_fusion.6), channel_id=1, source_target_pairs={{0,8},{2,10},{4,12},{6,14},{8,0},{10,2},{12,4},{14,6},{16,24},{18,... | collective-permute-start | bytes 3145736 | tf_op jit(solution)/shard_map/ppermute | solution.py:34
  126.4 127.5 %collective-permute-start.6 = (bf16[768,1664]{1,0:T(8,128)(2,1)}, bf16[768,1664]{1,0:T(8,128)(2,1)}, u32[]{:S(2)}, u32[]{:S(2)}) collective-permute-start(bf16[768,1664]{1,0:T(8,128)(2,1)} %pad_maximum_fusion.1), channel_id=1, source_target_pairs={{0,4},{2,6},{4,0},{6,2},{8,12},{10,14},{12,8},{14,10},{16,20},{18,... | collective-permute-start | bytes 7667720 | tf_op jit(solution)/shard_map/ppermute | solution.py:34
  130.2 146.5 %collective-permute-start.14 = (bf16[1536,896]{1,0:T(8,128)(2,1)S(1)}, bf16[1536,896]{1,0:T(8,128)(2,1)}, u32[]{:S(2)}, u32[]{:S(2)}) collective-permute-start(bf16[1536,896]{1,0:T(8,128)(2,1)S(1)} %constant_dynamic-update-slice_fusion.4.refs_0_), channel_id=1, source_target_pairs={{0,2},{2,0},{4,6},{6,4},{8,10},{10,8},{12,14},{14,12},{16,18},{18,... | collective-permute-start | bytes 8257544 | tf_op jit(solution)/shard_map/ppermute | solution.py:34
  175.1 136.7 %collective-permute-start.2 = (bf16[8192,128]{1,0:T(8,128)(2,1)}, bf16[8192,128]{1,0:T(8,128)(2,1)}, u32[]{:S(2)}, u32[]{:S(2)}) collective-permute-start(bf16[8192,128]{1,0:T(8,128)(2,1)} %pad_maximum_fusion.2), channel_id=1, source_target_pairs={{0,4},{2,6},{4,0},{6,2},{8,12},{10,14},{12,8},{14,10},{16,20},{18,... | collective-permute-start | bytes 6291464 | tf_op jit(solution)/shard_map/ppermute | solution.py:34
  176.3 60.8 %collective-permute-start.19 = (bf16[768,128]{1,0:T(8,128)(2,1)S(1)}, bf16[768,128]{1,0:T(8,128)(2,1)}, u32[]{:S(2)}, u32[]{:S(2)}) collective-permute-start(bf16[768,128]{1,0:T(8,128)(2,1)S(1)} %copy-done.122), channel_id=1, source_target_pairs={{0,4},{2,6},{4,0},{6,2},{8,12},{10,14},{12,8},{14,10},{16,20},{18,... | collective-permute-start | bytes 589832 | tf_op jit(solution)/shard_map/ppermute | solution.py:34
  183.4 56.8 %collective-permute-start.20 = (bf16[768,128]{1,0:T(8,128)(2,1)S(1)}, bf16[768,128]{1,0:T(8,128)(2,1)}, u32[]{:S(2)}, u32[]{:S(2)}) collective-permute-start(bf16[768,128]{1,0:T(8,128)(2,1)S(1)} %copy-done.121), channel_id=1, source_target_pairs={{0,20},{2,22},{4,16},{6,18},{8,28},{10,30},{12,24},{14,26},{16,4},... | collective-permute-start | bytes 589832 | tf_op jit(solution)/shard_map/ppermute | solution.py:34
  258.7 209.2 %collective-permute-start.7 = (bf16[1536,1664]{1,0:T(8,128)(2,1)}, bf16[1536,1664]{1,0:T(8,128)(2,1)}, u32[]{:S(2)}, u32[]{:S(2)}) collective-permute-start(bf16[1536,1664]{1,0:T(8,128)(2,1)} %constant_dynamic-update-slice_fusion.refs_0_), channel_id=1, source_target_pairs={{0,2},{2,0},{4,6},{6,4},{8,10},{10,8},{12,14},{14,12},{16,18},{18,... | collective-permute-start | bytes 15335432 | tf_op jit(solution)/shard_map/ppermute | solution.py:34
  310.6 45.7 %collective-permute-start.48 = (bf16[768,128]{1,0:T(8,128)(2,1)}, bf16[768,128]{1,0:T(8,128)(2,1)S(1)}, u32[]{:S(2)}, u32[]{:S(2)}) collective-permute-start(bf16[768,128]{1,0:T(8,128)(2,1)} %get-tuple-element.372), channel_id=1, source_target_pairs={{0,24},{2,26},{4,28},{6,30},{8,16},{10,18},{12,20},{14,22},{16,8},... | collective-permute-start | bytes 589832 | tf_op jit(solution)/shard_map/ppermute | solution.py:34
  311.7 46.2 %collective-permute-start.49 = (bf16[768,128]{1,0:T(8,128)(2,1)}, bf16[768,128]{1,0:T(8,128)(2,1)S(1)}, u32[]{:S(2)}, u32[]{:S(2)}) collective-permute-start(bf16[768,128]{1,0:T(8,128)(2,1)} %get-tuple-element.373), channel_id=1, source_target_pairs={{0,4},{2,6},{4,0},{6,2},{8,12},{10,14},{12,8},{14,10},{16,20},{18,... | collective-permute-start | bytes 589832 | tf_op jit(solution)/shard_map/ppermute | solution.py:34
  318.8 39.2 %collective-permute-start.50 = (bf16[768,128]{1,0:T(8,128)(2,1)}, bf16[768,128]{1,0:T(8,128)(2,1)S(1)}, u32[]{:S(2)}, u32[]{:S(2)}) collective-permute-start(bf16[768,128]{1,0:T(8,128)(2,1)} %get-tuple-element.374), channel_id=1, source_target_pairs={{0,20},{2,22},{4,16},{6,18},{8,28},{10,30},{12,24},{14,26},{16,4},... | collective-permute-start | bytes 589832 | tf_op jit(solution)/shard_map/ppermute | solution.py:34
  455.9 322.8 %collective-permute-start.3 = (bf16[16384,128]{1,0:T(8,128)(2,1)}, bf16[16384,128]{1,0:T(8,128)(2,1)}, u32[]{:S(2)}, u32[]{:S(2)}) collective-permute-start(bf16[16384,128]{1,0:T(8,128)(2,1)} %pad_maximum_fusion), channel_id=1, source_target_pairs={{0,2},{2,0},{4,6},{6,4},{8,10},{10,8},{12,14},{14,12},{16,18},{18,... | collective-permute-start | bytes 12582920 | tf_op jit(solution)/shard_map/ppermute | solution.py:34
  456.6 47.9 %collective-permute-start.53 = (bf16[768,128]{1,0:T(8,128)(2,1)}, bf16[768,128]{1,0:T(8,128)(2,1)S(1)}, u32[]{:S(2)}, u32[]{:S(2)}) collective-permute-start(bf16[768,128]{1,0:T(8,128)(2,1)} %get-tuple-element.377), channel_id=1, source_target_pairs={{0,2},{2,0},{4,6},{6,4},{8,10},{10,8},{12,14},{14,12},{16,18},{18,... | collective-permute-start | bytes 589832 | tf_op jit(solution)/shard_map/ppermute | solution.py:34
  456.7 49.4 %collective-permute-start.54 = (bf16[768,128]{1,0:T(8,128)(2,1)}, bf16[768,128]{1,0:T(8,128)(2,1)S(1)}, u32[]{:S(2)}, u32[]{:S(2)}) collective-permute-start(bf16[768,128]{1,0:T(8,128)(2,1)} %get-tuple-element.378), channel_id=1, source_target_pairs={{0,18},{2,16},{4,22},{6,20},{8,26},{10,24},{12,30},{14,28},{16,2},... | collective-permute-start | bytes 589832 | tf_op jit(solution)/shard_map/ppermute | solution.py:34
  467.9 41.9 %collective-permute-start.55 = (bf16[768,128]{1,0:T(8,128)(2,1)}, bf16[768,128]{1,0:T(8,128)(2,1)S(1)}, u32[]{:S(2)}, u32[]{:S(2)}) collective-permute-start(bf16[768,128]{1,0:T(8,128)(2,1)} %get-tuple-element.379), channel_id=1, source_target_pairs={{0,10},{2,8},{4,14},{6,12},{8,2},{10,0},{12,6},{14,4},{16,26},{18,... | collective-permute-start | bytes 589832 | tf_op jit(solution)/shard_map/ppermute | solution.py:34
  467.9 42.0 %collective-permute-start.56 = (bf16[768,128]{1,0:T(8,128)(2,1)}, bf16[768,128]{1,0:T(8,128)(2,1)S(1)}, u32[]{:S(2)}, u32[]{:S(2)}) collective-permute-start(bf16[768,128]{1,0:T(8,128)(2,1)} %get-tuple-element.380), channel_id=1, source_target_pairs={{0,26},{2,24},{4,30},{6,28},{8,18},{10,16},{12,22},{14,20},{16,10}... | collective-permute-start | bytes 589832 | tf_op jit(solution)/shard_map/ppermute | solution.py:34
  504.6 39.0 %collective-permute-start.57 = (bf16[768,128]{1,0:T(8,128)(2,1)}, bf16[768,128]{1,0:T(8,128)(2,1)S(1)}, u32[]{:S(2)}, u32[]{:S(2)}) collective-permute-start(bf16[768,128]{1,0:T(8,128)(2,1)} %get-tuple-element.381), channel_id=1, source_target_pairs={{0,6},{2,4},{4,2},{6,0},{8,14},{10,12},{12,10},{14,8},{16,22},{18,... | collective-permute-start | bytes 589832 | tf_op jit(solution)/shard_map/ppermute | solution.py:34
  577.2 46.2 %collective-permute-start.61 = (bf16[1280,128]{1,0:T(8,128)(2,1)S(1)}, bf16[1280,128]{1,0:T(8,128)(2,1)S(1)}, u32[]{:S(2)}, u32[]{:S(2)}) collective-permute-start(bf16[1280,128]{1,0:T(8,128)(2,1)S(1)} %copy-done.105), channel_id=1, source_target_pairs={{0,16},{2,18},{4,20},{6,22},{8,24},{10,26},{12,28},{14,30},{16,0},... | collective-permute-start | bytes 983048 | tf_op jit(solution)/shard_map/ppermute | solution.py:34
  577.3 46.3 %collective-permute-start.62 = (bf16[1280,128]{1,0:T(8,128)(2,1)S(1)}, bf16[1280,128]{1,0:T(8,128)(2,1)S(1)}, u32[]{:S(2)}, u32[]{:S(2)}) collective-permute-start(bf16[1280,128]{1,0:T(8,128)(2,1)S(1)} %copy-done.104), channel_id=1, source_target_pairs={{0,8},{2,10},{4,12},{6,14},{8,0},{10,2},{12,4},{14,6},{16,24},{18,... | collective-permute-start | bytes 983048 | tf_op jit(solution)/shard_map/ppermute | solution.py:34
  699.1 44.6 %collective-permute-start.83 = (bf16[1024,128]{1,0:T(8,128)(2,1)}, bf16[1024,128]{1,0:T(8,128)(2,1)S(1)}, u32[]{:S(2)}, u32[]{:S(2)}) collective-permute-start(bf16[1024,128]{1,0:T(8,128)(2,1)} %get-tuple-element.443), channel_id=1, source_target_pairs={{0,2},{2,0},{4,6},{6,4},{8,10},{10,8},{12,14},{14,12},{16,18},{18,... | collective-permute-start | bytes 786440 | tf_op jit(solution)/shard_map/ppermute | solution.py:34
  701.0 44.8 %collective-permute-start.84 = (bf16[1024,128]{1,0:T(8,128)(2,1)}, bf16[1024,128]{1,0:T(8,128)(2,1)S(1)}, u32[]{:S(2)}, u32[]{:S(2)}) collective-permute-start(bf16[1024,128]{1,0:T(8,128)(2,1)} %get-tuple-element.444), channel_id=1, source_target_pairs={{0,18},{2,16},{4,22},{6,20},{8,26},{10,24},{12,30},{14,28},{16,2},... | collective-permute-start | bytes 786440 | tf_op jit(solution)/shard_map/ppermute | solution.py:34
  704.8 41.2 %collective-permute-start.85 = (bf16[1024,128]{1,0:T(8,128)(2,1)}, bf16[1024,128]{1,0:T(8,128)(2,1)S(1)}, u32[]{:S(2)}, u32[]{:S(2)}) collective-permute-start(bf16[1024,128]{1,0:T(8,128)(2,1)} %get-tuple-element.445), channel_id=1, source_target_pairs={{0,10},{2,8},{4,14},{6,12},{8,2},{10,0},{12,6},{14,4},{16,26},{18,... | collective-permute-start | bytes 786440 | tf_op jit(solution)/shard_map/ppermute | solution.py:34
  (245 other events, 7252.1 us)

commit v5 on v4

--- a/solution.py
+++ b/solution.py
@@ -12,6 +12,8 @@
 SUBLANES = 16
 WEIGHTS = (6, 8, 6, 10, 8, 4, 3)
 GROUPS = (0, 1, 3)
+SLICE = 1536
+PER_STEP = 4
 VMEM = 60 * 1024 * 1024
 
 
@@ -94,7 +96,7 @@
 def rotate_kernel(columns, part, grads, order, me_ref, *refs):
     own_ref, other_ref, grad_ref = refs[:3]
     outs = refs[3 : 3 + len(order)]
-    stage, basis_t, rows, pair = refs[-4:]
+    stage, basis_t, rows = refs[-3:]
     step = pl.program_id(0)
     pitch = full_rows(part)
 
@@ -115,11 +117,16 @@
 
         lax.fori_loop(0, stage.shape[1] // LANES, turned, 0)
 
-    pair[:, :LANES] = grad_ref[0].astype(jnp.bfloat16)
-    pair[:, LANES:] = grad_ref[1].astype(jnp.bfloat16)
-    product = jnp.dot(basis_t[:columns, :], pair[...], preferred_element_type=jnp.float32)
-    for half in range(2):
-        rows[pl.ds(2 * step + half, columns, stride=grads), :] = product[:, half * LANES : (half + 1) * LANES]
+    for first in range(0, PER_STEP, 2):
+        product = None
+        for low in range(0, grad_ref.shape[1], SLICE):
+            depth = slice(low, min(low + SLICE, grad_ref.shape[1]))
+            pair = jnp.concatenate([grad_ref[first + half, depth, :].astype(jnp.bfloat16) for half in range(2)], axis=1)
+            term = jnp.dot(basis_t[:columns, depth], pair, preferred_element_type=jnp.float32)
+            product = term if product is None else product + term
+        for half in range(2):
+            place = pl.ds(PER_STEP * step + first + half, columns, stride=grads)
+            rows[place, :] = product[:, half * LANES : (half + 1) * LANES]
 
     @pl.when(step == pl.num_programs(0) - 1)
     def _():
@@ -142,14 +149,13 @@
         functools.partial(rotate_kernel, columns, part, grads, order),
         grid_spec=pltpu.PrefetchScalarGridSpec(
             num_scalar_prefetch=1,
-            grid=(grads // 2,),
-            in_specs=[basis_spec, basis_spec, pl.BlockSpec((2, depth, LANES), lambda step, me: (step, 0, 0))],
+            grid=(grads // PER_STEP,),
+            in_specs=[basis_spec, basis_spec, pl.BlockSpec((PER_STEP, depth, LANES), lambda step, me: (step, 0, 0))],
             out_specs=[pl.BlockSpec((height, LANES), lambda step, me: (0, 0))] * devices,
             scratch_shapes=[
                 pltpu.VMEM((depth, wide), jnp.float32),
                 pltpu.VMEM((wide, depth), jnp.bfloat16),
                 pltpu.VMEM((columns * grads, LANES), jnp.float32),
-                pltpu.VMEM((depth, 2 * LANES), jnp.bfloat16),
             ],
         ),
         out_shape=[jax.ShapeDtypeStruct((height, LANES), jnp.bfloat16)] * devices,

time: 918 us -> 885 us (0.964)
  Pallas kernels: 317 us -> 280 us
    pallas_call x7, Pallas kernels: 215 us -> 179 us  [rotate(): pl.pallas_call(functools.partial(rotate_kernel, columns, part, grads, ord...]
  transfers between devices with their start and end apart: 121 -> 121, of which waited for: 32 -> 34; matrix products, arithmetic and copies ran while one was open for 4% -> 4% of each run, Pallas kernels for 34% -> 31%
where the time goes in v5:
time: 885 us; the launch traced here: 876 us
  waiting for transfers between devices  386 us (44%)
  Pallas kernels  280 us (32%)
  starting transfers between devices  169 us (19%)
  other arithmetic  22.8 us (3%)
  local copies, waits for them, and re-layouts  16.2 us (2%)
    ppermute x121, waiting for transfers between devices, exchange(): lax.ppermute(block, 'rows', [(source, source ^ flip) for source in range(...  386 us
    pallas_call x7, Pallas kernels, rotate(): pl.pallas_call(functools.partial(rotate_kernel, columns, part, grads, ord...  179 us
    ppermute x121, starting transfers between devices, exchange(): lax.ppermute(block, 'rows', [(source, source ^ flip) for source in range(...  169 us
    pallas_call x7, Pallas kernels, finish(): pl.pallas_call(functools.partial(finish_kernel, begin, grads, devices), g...  86.8 us
    concatenate x10, other arithmetic, spread(): block = jnp.concatenate([block, other])  22.8 us
  transfers between devices with their start and end apart: 121, of which 34 were waited for; matrix products, arithmetic and copies ran while one was open for 4% of the time, Pallas kernels for 31%

profile of v5, /device:TPU:11, one launch (start us, length us, event | category | flops | bytes accessed | tf_op | source)
XLA Modules:
  0.0 875.6 jit_solution(5178658920229787008)
XLA Ops:
  36.3 21.2 %collective-permute-done.8 = bf16[192,896]{1,0:T(8,128)(2,1)S(1)} collective-permute-done((bf16[192,896]{1,0:T(8,128)(2,1)}, bf16[192,896]{1,0:T(8,128)(2,1)S(1)}, u32[]{:S(2)}, u32[]{:S(2)}) %collective-permute-start.8) | collective-permute-done | bytes 344096 | tf_op jit(solution)/shard_map/ppermute | solution.py:36
  58.7 12.5 %collective-permute-done.4 = bf16[192,1664]{1,0:T(8,128)(2,1)S(1)} collective-permute-done((bf16[192,1664]{1,0:T(8,128)(2,1)}, bf16[192,1664]{1,0:T(8,128)(2,1)S(1)}, u32[]{:S(2)}, u32[]{:S(2)}) %collective-permute-start.4) | collective-permute-done | bytes 639008 | tf_op jit(solution)/shard_map/ppermute | solution.py:36
  78.3 17.6 %collective-permute-done.12 = bf16[384,896]{1,0:T(8,128)(2,1)S(1)} collective-permute-done((bf16[384,896]{1,0:T(8,128)(2,1)S(1)}, bf16[384,896]{1,0:T(8,128)(2,1)S(1)}, u32[]{:S(2)}, u32[]{:S(2)}) %collective-permute-start.12) | collective-permute-done | bytes 688160 | tf_op jit(solution)/shard_map/ppermute | solution.py:36
  101.2 14.5 %collective-permute-done = bf16[2048,128]{1,0:T(8,128)(2,1)} collective-permute-done((bf16[2048,128]{1,0:T(8,128)(2,1)}, bf16[2048,128]{1,0:T(8,128)(2,1)}, u32[]{:S(2)}, u32[]{:S(2)}) %collective-permute-start) | collective-permute-done | bytes 524320 | tf_op jit(solution)/shard_map/ppermute | solution.py:36
  132.0 24.8 %shard_map.52 = (bf16[768,128]{1,0:T(8,128)(2,1)}, bf16[768,128]{1,0:T(8,128)(2,1)}, bf16[768,128]{1,0:T(8,128)(2,1)}, bf16[768,128]{1,0:T(8,128)(2,1)}, bf16[76...) custom-call(s32[1]{0:T(128)} %bitcast.2.me_ref, ...), custom_call_target="tpu_custom_call" | custom-call | flops 9059696640 | bytes 52543488 | tf_op jit(solution)/shard_map/pallas_call | solution.py:148
  178.8 58.2 %collective-permute-done.19.refs_7_ = bf16[768,128]{1,0:T(8,128)(2,1)} collective-permute-done((bf16[768,128]{1,0:T(8,128)(2,1)S(1)}, bf16[768,128]{1,0:T(8,128)(2,1)}, u32[]{:S(2)}, u32[]{:S(2)}) %collective-permute-start.19) | collective-permute-done | bytes 196640 | tf_op jit(solution)/shard_map/ppermute | solution.py:36
  279.2 24.4 %shard_map.51 = (bf16[768,128]{1,0:T(8,128)(2,1)}, bf16[768,128]{1,0:T(8,128)(2,1)}, bf16[768,128]{1,0:T(8,128)(2,1)}, bf16[768,128]{1,0:T(8,128)(2,1)}, bf16[76...) custom-call(s32[1]{0:T(128)} %bitcast.2.me_ref, ...), custom_call_target="tpu_custom_call" | custom-call | flops 9059696640 | bytes 52543488 | tf_op jit(solution)/shard_map/pallas_call | solution.py:148
  317.8 28.1 %shard_map.54 = (bf16[1024,128]{1,0:T(8,128)(2,1)}, bf16[1024,128]{1,0:T(8,128)(2,1)}, bf16[1024,128]{1,0:T(8,128)(2,1)}, bf16[1024,128]{1,0:T(8,128)(2,1)}, bf1...) custom-call(s32[1]{0:T(128)} %bitcast.2.me_ref, ...), custom_call_target="tpu_custom_call" | custom-call | flops 12079595520 | bytes 54329344 | tf_op jit(solution)/shard_map/pallas_call | solution.py:148
  350.6 29.9 %collective-permute-done.52.refs_10_ = bf16[768,128]{1,0:T(8,128)(2,1)S(1)} collective-permute-done((bf16[768,128]{1,0:T(8,128)(2,1)S(1)}, bf16[768,128]{1,0:T(8,128)(2,1)S(1)}, u32[]{:S(2)}, u32[]{:S(2)}) %collective-permute-start.52) | collective-permute-done | bytes 196640 | tf_op jit(solution)/shard_map/ppermute | solution.py:36
  386.0 16.7 %collective-permute-done.34.refs_7_ = bf16[1024,128]{1,0:T(8,128)(2,1)S(1)} collective-permute-done((bf16[1024,128]{1,0:T(8,128)(2,1)}, bf16[1024,128]{1,0:T(8,128)(2,1)S(1)}, u32[]{:S(2)}, u32[]{:S(2)}) %collective-permute-start.34) | collective-permute-done | bytes 262176 | tf_op jit(solution)/shard_map/ppermute | solution.py:36
  420.5 15.4 %collective-permute-done.41.refs_14_ = bf16[1024,128]{1,0:T(8,128)(2,1)S(1)} collective-permute-done((bf16[1024,128]{1,0:T(8,128)(2,1)}, bf16[1024,128]{1,0:T(8,128)(2,1)S(1)}, u32[]{:S(2)}, u32[]{:S(2)}) %collective-permute-start.41) | collective-permute-done | bytes 262176 | tf_op jit(solution)/shard_map/ppermute | solution.py:36
  457.6 32.3 %shard_map.53 = (bf16[1280,128]{1,0:T(8,128)(2,1)}, bf16[1280,128]{1,0:T(8,128)(2,1)}, bf16[1280,128]{1,0:T(8,128)(2,1)}, bf16[1280,128]{1,0:T(8,128)(2,1)}, bf1...) custom-call(s32[1]{0:T(128)} %bitcast.2.me_ref, ...), custom_call_target="tpu_custom_call" | custom-call | flops 15099494400 | bytes 56115200 | tf_op jit(solution)/shard_map/pallas_call | solution.py:148
  495.6 28.1 %shard_map.55 = (bf16[1024,128]{1,0:T(8,128)(2,1)}, bf16[1024,128]{1,0:T(8,128)(2,1)}, bf16[1024,128]{1,0:T(8,128)(2,1)}, bf16[1024,128]{1,0:T(8,128)(2,1)}, bf1...) custom-call(s32[1]{0:T(128)} %bitcast.2.me_ref, ...), custom_call_target="tpu_custom_call" | custom-call | flops 12079595520 | bytes 54329344 | tf_op jit(solution)/shard_map/pallas_call | solution.py:148
  545.1 12.3 %collective-permute-done.78.refs_6_ = bf16[1024,128]{1,0:T(8,128)(2,1)S(1)} collective-permute-done((bf16[1024,128]{1,0:T(8,128)(2,1)}, bf16[1024,128]{1,0:T(8,128)(2,1)S(1)}, u32[]{:S(2)}, u32[]{:S(2)}) %collective-permute-start.78) | collective-permute-done | bytes 262176 | tf_op jit(solution)/shard_map/ppermute | solution.py:36
  570.8 32.2 %collective-permute-done.82.refs_10_ = bf16[1024,128]{1,0:T(8,128)(2,1)} collective-permute-done((bf16[1024,128]{1,0:T(8,128)(2,1)}, bf16[1024,128]{1,0:T(8,128)(2,1)}, u32[]{:S(2)}, u32[]{:S(2)}) %collective-permute-start.82) | collective-permute-done | bytes 262176 | tf_op jit(solution)/shard_map/ppermute | solution.py:36
  607.9 20.4 %collective-permute-done.64.refs_7_ = bf16[1280,128]{1,0:T(8,128)(2,1)S(1)} collective-permute-done((bf16[1280,128]{1,0:T(8,128)(2,1)S(1)}, bf16[1280,128]{1,0:T(8,128)(2,1)S(1)}, u32[]{:S(2)}, u32[]{:S(2)}) %collective-permute-start.64) | collective-permute-done | bytes 327712 | tf_op jit(solution)/shard_map/ppermute | solution.py:36
  650.1 22.4 %collective-permute-done.71.refs_14_ = bf16[1280,128]{1,0:T(8,128)(2,1)} collective-permute-done((bf16[1280,128]{1,0:T(8,128)(2,1)}, bf16[1280,128]{1,0:T(8,128)(2,1)}, u32[]{:S(2)}, u32[]{:S(2)}) %collective-permute-start.71) | collective-permute-done | bytes 327712 | tf_op jit(solution)/shard_map/ppermute | solution.py:36
  697.0 21.1 %shard_map.56 = (bf16[512,128]{1,0:T(8,128)(2,1)}, bf16[512,128]{1,0:T(8,128)(2,1)}, bf16[512,128]{1,0:T(8,128)(2,1)}, bf16[512,128]{1,0:T(8,128)(2,1)}, bf16[51...) custom-call(s32[1]{0:T(128)} %bitcast.2.me_ref, ...), custom_call_target="tpu_custom_call" | custom-call | flops 6039797760 | bytes 50757632 | tf_op jit(solution)/shard_map/pallas_call | solution.py:148
  724.1 19.9 %shard_map.57 = (bf16[384,128]{1,0:T(8,128)(2,1)}, bf16[384,128]{1,0:T(8,128)(2,1)}, bf16[384,128]{1,0:T(8,128)(2,1)}, bf16[384,128]{1,0:T(8,128)(2,1)}, bf16[38...) custom-call(s32[1]{0:T(128)} %bitcast.2.me_ref, ...), custom_call_target="tpu_custom_call" | custom-call | flops 4529848320 | bytes 49864704 | tf_op jit(solution)/shard_map/pallas_call | solution.py:148
  750.4 12.0 %shard_map.58.refs_19_ = f32[2048,5760]{1,0:T(8,128)} custom-call(bf16[8,2048,128]{2,1,0:T(8,128)(2,1)} %bitcast.refs_0_, bf16[8,2048,128]{2,1,0:T(8,128)(2,1)} %bitcast.1.refs_1_, f32[2048,256]{1,0:T(8,128)} %shard_map.48.refs_2_, bf16[768,128]{1,0:T(8,128)(2,1)} %get-tuple-element.547.refs_3_, bf16[768,128]{1,0:T(8,128)(2,1)} %copy-done.59, ...), custom_call_target="tpu_custom_call" | custom-call | flops 6442450944 | bytes 17825792 | tf_op jit(solution)/shard_map/pallas_call | solution.py:208
  769.3 14.0 %shard_map.59.refs_19_ = f32[2048,5760]{1,0:T(8,128)} custom-call(bf16[8,2048,128]{2,1,0:T(8,128)(2,1)} %bitcast.refs_0_, bf16[8,2048,128]{2,1,0:T(8,128)(2,1)} %bitcast.1.refs_1_, f32[2048,256]{1,0:T(8,128)} %shard_map.48.refs_2_, bf16[1024,128]{1,0:T(8,128)(2,1)} %get-tuple-element.531.refs_3_, ...), custom_call_target="tpu_custom_call", output_to_operand_aliasing={{}: (19, {})} | custom-call | flops 8589934592 | bytes 20971520 | tf_op jit(solution)/shard_map/pallas_call | solution.py:208
  790.3 11.7 %shard_map.60.refs_19_ = f32[2048,5760]{1,0:T(8,128)} custom-call(bf16[8,2048,128]{2,1,0:T(8,128)(2,1)} %bitcast.refs_0_, bf16[8,2048,128]{2,1,0:T(8,128)(2,1)} %bitcast.1.refs_1_, f32[2048,256]{1,0:T(8,128)} %shard_map.48.refs_2_, bf16[768,128]{1,0:T(8,128)(2,1)} %get-tuple-element.515.refs_3_, ...), custom_call_target="tpu_custom_call", output_to_operand_aliasing={{}: (19, {})} | custom-call | flops 6442450944 | bytes 17825792 | tf_op jit(solution)/shard_map/pallas_call | solution.py:208
  808.8 16.6 %shard_map.61.refs_19_ = f32[2048,5760]{1,0:T(8,128)} custom-call(bf16[8,2048,128]{2,1,0:T(8,128)(2,1)} %bitcast.refs_0_, bf16[8,2048,128]{2,1,0:T(8,128)(2,1)} %bitcast.1.refs_1_, f32[2048,256]{1,0:T(8,128)} %shard_map.48.refs_2_, bf16[1280,128]{1,0:T(8,128)(2,1)} %get-tuple-element.499.refs_3_, ...), custom_call_target="tpu_custom_call", output_to_operand_aliasing={{}: (19, {})} | custom-call | flops 10737418240 | bytes 24117248 | tf_op jit(solution)/shard_map/pallas_call | solution.py:208
  832.9 14.0 %shard_map.62.refs_19_ = f32[2048,5760]{1,0:T(8,128)} custom-call(bf16[8,2048,128]{2,1,0:T(8,128)(2,1)} %bitcast.refs_0_, bf16[8,2048,128]{2,1,0:T(8,128)(2,1)} %bitcast.1.refs_1_, f32[2048,256]{1,0:T(8,128)} %shard_map.48.refs_2_, bf16[1024,128]{1,0:T(8,128)(2,1)} %get-tuple-element.483.refs_3_, ...), custom_call_target="tpu_custom_call", output_to_operand_aliasing={{}: (19, {})} | custom-call | flops 8589934592 | bytes 20971520 | tf_op jit(solution)/shard_map/pallas_call | solution.py:208
  (551 shorter events, 353.3 us)
Async XLA Ops:
  28.3 42.9 %collective-permute-start.4 = (bf16[192,1664]{1,0:T(8,128)(2,1)}, bf16[192,1664]{1,0:T(8,128)(2,1)S(1)}, u32[]{:S(2)}, u32[]{:S(2)}) collective-permute-start(bf16[192,1664]{1,0:T(8,128)(2,1)} %get-tuple-element.284), channel_id=1, source_target_pairs={{0,16},{2,18},{4,20},{6,22},{8,24},{10,26},{12,28},{14,30},{16,0},... | collective-permute-start | bytes 1916936 | tf_op jit(solution)/shard_map/ppermute | solution.py:36
  58.6 37.2 %collective-permute-start.12 = (bf16[384,896]{1,0:T(8,128)(2,1)S(1)}, bf16[384,896]{1,0:T(8,128)(2,1)S(1)}, u32[]{:S(2)}, u32[]{:S(2)}) collective-permute-start(bf16[384,896]{1,0:T(8,128)(2,1)S(1)} %pad_maximum_fusion.7), channel_id=1, source_target_pairs={{0,8},{2,10},{4,12},{6,14},{8,0},{10,2},{12,4},{14,6},{16,24},{18,... | collective-permute-start | bytes 2064392 | tf_op jit(solution)/shard_map/ppermute | solution.py:36
  73.3 50.1 %collective-permute-start.5 = (bf16[384,1664]{1,0:T(8,128)(2,1)}, bf16[384,1664]{1,0:T(8,128)(2,1)}, u32[]{:S(2)}, u32[]{:S(2)}) collective-permute-start(bf16[384,1664]{1,0:T(8,128)(2,1)} %pad_maximum_fusion.4), channel_id=1, source_target_pairs={{0,8},{2,10},{4,12},{6,14},{8,0},{10,2},{12,4},{14,6},{16,24},{18,... | collective-permute-start | bytes 3833864 | tf_op jit(solution)/shard_map/ppermute | solution.py:36
  75.3 40.4 %collective-permute-start = (bf16[2048,128]{1,0:T(8,128)(2,1)}, bf16[2048,128]{1,0:T(8,128)(2,1)}, u32[]{:S(2)}, u32[]{:S(2)}) collective-permute-start(bf16[2048,128]{1,0:T(8,128)(2,1)} %shard_map.46), channel_id=1, source_target_pairs={{0,16},{2,18},{4,20},{6,22},{8,24},{10,26},{12,28},{14,30},{16,0},... | collective-permute-start | bytes 1572872 | tf_op jit(solution)/shard_map/ppermute | solution.py:36
  117.8 43.4 %collective-permute-start.1 = (bf16[4096,128]{1,0:T(8,128)(2,1)}, bf16[4096,128]{1,0:T(8,128)(2,1)}, u32[]{:S(2)}, u32[]{:S(2)}) collective-permute-start(bf16[4096,128]{1,0:T(8,128)(2,1)} %pad_maximum_fusion.6), channel_id=1, source_target_pairs={{0,8},{2,10},{4,12},{6,14},{8,0},{10,2},{12,4},{14,6},{16,24},{18,... | collective-permute-start | bytes 3145736 | tf_op jit(solution)/shard_map/ppermute | solution.py:36
  126.4 127.5 %collective-permute-start.6 = (bf16[768,1664]{1,0:T(8,128)(2,1)}, bf16[768,1664]{1,0:T(8,128)(2,1)}, u32[]{:S(2)}, u32[]{:S(2)}) collective-permute-start(bf16[768,1664]{1,0:T(8,128)(2,1)} %pad_maximum_fusion.1), channel_id=1, source_target_pairs={{0,4},{2,6},{4,0},{6,2},{8,12},{10,14},{12,8},{14,10},{16,20},{18,... | collective-permute-start | bytes 7667720 | tf_op jit(solution)/shard_map/ppermute | solution.py:36
  130.2 146.5 %collective-permute-start.14 = (bf16[1536,896]{1,0:T(8,128)(2,1)S(1)}, bf16[1536,896]{1,0:T(8,128)(2,1)}, u32[]{:S(2)}, u32[]{:S(2)}) collective-permute-start(bf16[1536,896]{1,0:T(8,128)(2,1)S(1)} %constant_dynamic-update-slice_fusion.4.refs_0_), channel_id=1, source_target_pairs={{0,2},{2,0},{4,6},{6,4},{8,10},{10,8},{12,14},{14,12},{16,18},{18,... | collective-permute-start | bytes 8257544 | tf_op jit(solution)/shard_map/ppermute | solution.py:36
  169.7 136.7 %collective-permute-start.2 = (bf16[8192,128]{1,0:T(8,128)(2,1)}, bf16[8192,128]{1,0:T(8,128)(2,1)}, u32[]{:S(2)}, u32[]{:S(2)}) collective-permute-start(bf16[8192,128]{1,0:T(8,128)(2,1)} %pad_maximum_fusion.2), channel_id=1, source_target_pairs={{0,4},{2,6},{4,0},{6,2},{8,12},{10,14},{12,8},{14,10},{16,20},{18,... | collective-permute-start | bytes 6291464 | tf_op jit(solution)/shard_map/ppermute | solution.py:36
  170.9 66.2 %collective-permute-start.19 = (bf16[768,128]{1,0:T(8,128)(2,1)S(1)}, bf16[768,128]{1,0:T(8,128)(2,1)}, u32[]{:S(2)}, u32[]{:S(2)}) collective-permute-start(bf16[768,128]{1,0:T(8,128)(2,1)S(1)} %copy-done.122), channel_id=1, source_target_pairs={{0,4},{2,6},{4,0},{6,2},{8,12},{10,14},{12,8},{14,10},{16,20},{18,... | collective-permute-start | bytes 589832 | tf_op jit(solution)/shard_map/ppermute | solution.py:36
  177.9 62.3 %collective-permute-start.20 = (bf16[768,128]{1,0:T(8,128)(2,1)S(1)}, bf16[768,128]{1,0:T(8,128)(2,1)}, u32[]{:S(2)}, u32[]{:S(2)}) collective-permute-start(bf16[768,128]{1,0:T(8,128)(2,1)S(1)} %copy-done.121), channel_id=1, source_target_pairs={{0,20},{2,22},{4,16},{6,18},{8,28},{10,30},{12,24},{14,26},{16,4},... | collective-permute-start | bytes 589832 | tf_op jit(solution)/shard_map/ppermute | solution.py:36
  258.7 198.8 %collective-permute-start.7 = (bf16[1536,1664]{1,0:T(8,128)(2,1)}, bf16[1536,1664]{1,0:T(8,128)(2,1)}, u32[]{:S(2)}, u32[]{:S(2)}) collective-permute-start(bf16[1536,1664]{1,0:T(8,128)(2,1)} %constant_dynamic-update-slice_fusion.refs_0_), channel_id=1, source_target_pairs={{0,2},{2,0},{4,6},{6,4},{8,10},{10,8},{12,14},{14,12},{16,18},{18,... | collective-permute-start | bytes 15335432 | tf_op jit(solution)/shard_map/ppermute | solution.py:36
  305.3 40.6 %collective-permute-start.48 = (bf16[768,128]{1,0:T(8,128)(2,1)}, bf16[768,128]{1,0:T(8,128)(2,1)S(1)}, u32[]{:S(2)}, u32[]{:S(2)}) collective-permute-start(bf16[768,128]{1,0:T(8,128)(2,1)} %get-tuple-element.372), channel_id=1, source_target_pairs={{0,24},{2,26},{4,28},{6,30},{8,16},{10,18},{12,20},{14,22},{16,8},... | collective-permute-start | bytes 589832 | tf_op jit(solution)/shard_map/ppermute | solution.py:36
  306.4 41.1 %collective-permute-start.49 = (bf16[768,128]{1,0:T(8,128)(2,1)}, bf16[768,128]{1,0:T(8,128)(2,1)S(1)}, u32[]{:S(2)}, u32[]{:S(2)}) collective-permute-start(bf16[768,128]{1,0:T(8,128)(2,1)} %get-tuple-element.373), channel_id=1, source_target_pairs={{0,4},{2,6},{4,0},{6,2},{8,12},{10,14},{12,8},{14,10},{16,20},{18,... | collective-permute-start | bytes 589832 | tf_op jit(solution)/shard_map/ppermute | solution.py:36
  445.3 302.8 %collective-permute-start.3 = (bf16[16384,128]{1,0:T(8,128)(2,1)}, bf16[16384,128]{1,0:T(8,128)(2,1)}, u32[]{:S(2)}, u32[]{:S(2)}) collective-permute-start(bf16[16384,128]{1,0:T(8,128)(2,1)} %pad_maximum_fusion), channel_id=1, source_target_pairs={{0,2},{2,0},{4,6},{6,4},{8,10},{10,8},{12,14},{14,12},{16,18},{18,... | collective-permute-start | bytes 12582920 | tf_op jit(solution)/shard_map/ppermute | solution.py:36
  446.0 43.9 %collective-permute-start.53 = (bf16[768,128]{1,0:T(8,128)(2,1)}, bf16[768,128]{1,0:T(8,128)(2,1)S(1)}, u32[]{:S(2)}, u32[]{:S(2)}) collective-permute-start(bf16[768,128]{1,0:T(8,128)(2,1)} %get-tuple-element.377), channel_id=1, source_target_pairs={{0,2},{2,0},{4,6},{6,4},{8,10},{10,8},{12,14},{14,12},{16,18},{18,... | collective-permute-start | bytes 589832 | tf_op jit(solution)/shard_map/ppermute | solution.py:36
  446.2 45.3 %collective-permute-start.54 = (bf16[768,128]{1,0:T(8,128)(2,1)}, bf16[768,128]{1,0:T(8,128)(2,1)S(1)}, u32[]{:S(2)}, u32[]{:S(2)}) collective-permute-start(bf16[768,128]{1,0:T(8,128)(2,1)} %get-tuple-element.378), channel_id=1, source_target_pairs={{0,18},{2,16},{4,22},{6,20},{8,26},{10,24},{12,30},{14,28},{16,2},... | collective-permute-start | bytes 589832 | tf_op jit(solution)/shard_map/ppermute | solution.py:36
  457.5 37.8 %collective-permute-start.55 = (bf16[768,128]{1,0:T(8,128)(2,1)}, bf16[768,128]{1,0:T(8,128)(2,1)S(1)}, u32[]{:S(2)}, u32[]{:S(2)}) collective-permute-start(bf16[768,128]{1,0:T(8,128)(2,1)} %get-tuple-element.379), channel_id=1, source_target_pairs={{0,10},{2,8},{4,14},{6,12},{8,2},{10,0},{12,6},{14,4},{16,26},{18,... | collective-permute-start | bytes 589832 | tf_op jit(solution)/shard_map/ppermute | solution.py:36
  457.5 37.8 %collective-permute-start.56 = (bf16[768,128]{1,0:T(8,128)(2,1)}, bf16[768,128]{1,0:T(8,128)(2,1)S(1)}, u32[]{:S(2)}, u32[]{:S(2)}) collective-permute-start(bf16[768,128]{1,0:T(8,128)(2,1)} %get-tuple-element.380), channel_id=1, source_target_pairs={{0,26},{2,24},{4,30},{6,28},{8,18},{10,16},{12,22},{14,20},{16,10}... | collective-permute-start | bytes 589832 | tf_op jit(solution)/shard_map/ppermute | solution.py:36
  557.4 46.2 %collective-permute-start.61 = (bf16[1280,128]{1,0:T(8,128)(2,1)S(1)}, bf16[1280,128]{1,0:T(8,128)(2,1)S(1)}, u32[]{:S(2)}, u32[]{:S(2)}) collective-permute-start(bf16[1280,128]{1,0:T(8,128)(2,1)S(1)} %copy-done.105), channel_id=1, source_target_pairs={{0,16},{2,18},{4,20},{6,22},{8,24},{10,26},{12,28},{14,30},{16,0},... | collective-permute-start | bytes 983048 | tf_op jit(solution)/shard_map/ppermute | solution.py:36
  557.4 46.3 %collective-permute-start.62 = (bf16[1280,128]{1,0:T(8,128)(2,1)S(1)}, bf16[1280,128]{1,0:T(8,128)(2,1)S(1)}, u32[]{:S(2)}, u32[]{:S(2)}) collective-permute-start(bf16[1280,128]{1,0:T(8,128)(2,1)S(1)} %copy-done.104), channel_id=1, source_target_pairs={{0,8},{2,10},{4,12},{6,14},{8,0},{10,2},{12,4},{14,6},{16,24},{18,... | collective-permute-start | bytes 983048 | tf_op jit(solution)/shard_map/ppermute | solution.py:36
  568.5 37.8 %collective-permute-start.63 = (bf16[1280,128]{1,0:T(8,128)(2,1)S(1)}, bf16[1280,128]{1,0:T(8,128)(2,1)S(1)}, u32[]{:S(2)}, u32[]{:S(2)}) collective-permute-start(bf16[1280,128]{1,0:T(8,128)(2,1)S(1)} %copy-done.103), channel_id=1, source_target_pairs={{0,24},{2,26},{4,28},{6,30},{8,16},{10,18},{12,20},{14,22},{16,8},... | collective-permute-start | bytes 983048 | tf_op jit(solution)/shard_map/ppermute | solution.py:36
  633.6 38.8 %collective-permute-start.71 = (bf16[1280,128]{1,0:T(8,128)(2,1)}, bf16[1280,128]{1,0:T(8,128)(2,1)}, u32[]{:S(2)}, u32[]{:S(2)}) collective-permute-start(bf16[1280,128]{1,0:T(8,128)(2,1)} %get-tuple-element.413), channel_id=1, source_target_pairs={{0,26},{2,24},{4,30},{6,28},{8,18},{10,16},{12,22},{14,20},{16,10}... | collective-permute-start | bytes 983048 | tf_op jit(solution)/shard_map/ppermute | solution.py:36
  679.2 38.9 %collective-permute-start.83 = (bf16[1024,128]{1,0:T(8,128)(2,1)}, bf16[1024,128]{1,0:T(8,128)(2,1)S(1)}, u32[]{:S(2)}, u32[]{:S(2)}) collective-permute-start(bf16[1024,128]{1,0:T(8,128)(2,1)} %get-tuple-element.443), channel_id=1, source_target_pairs={{0,2},{2,0},{4,6},{6,4},{8,10},{10,8},{12,14},{14,12},{16,18},{18,... | collective-permute-start | bytes 786440 | tf_op jit(solution)/shard_map/ppermute | solution.py:36
  681.2 39.0 %collective-permute-start.84 = (bf16[1024,128]{1,0:T(8,128)(2,1)}, bf16[1024,128]{1,0:T(8,128)(2,1)S(1)}, u32[]{:S(2)}, u32[]{:S(2)}) collective-permute-start(bf16[1024,128]{1,0:T(8,128)(2,1)} %get-tuple-element.444), channel_id=1, source_target_pairs={{0,18},{2,16},{4,22},{6,20},{8,26},{10,24},{12,30},{14,28},{16,2},... | collective-permute-start | bytes 786440 | tf_op jit(solution)/shard_map/ppermute | solution.py:36
  (245 other events, 7093.7 us)
